TPU v7x, 128 devices: a whole 4x4x4 slice. The times are simulated.
128 devices in a mesh: cells: 128 (over x, z, y, core).
Axes of the slice: x: 4, y: 4, z: 4, core: 2. Of those that a mesh axis runs over, the one named last changes fastest.
Arguments:
- parcel_locations: float32 [3, 655360], P(None, 'cells'), may hold values from 0 to 1.2
- parcel_speed: float32 [3, 655360], P(None, 'cells'), may hold values from -6 to 6
- explicit_forcing: float32 [3, 655360], P(None, 'cells'), may hold values from -6 to 6
- parcel_weight: float32 [655360], P('cells'), may hold values from 0.5 to 2
- scaled_heat: float32 [655360], P('cells'), may hold values from 0 to 1
- solid_share: float32 [655360], P('cells'), may hold values from 0 to 0.4
- alive_tally: int32 [10240], P('cells'), may hold values from 1 to 64, as said below
- target_processor: int32 [10240], P('cells'), may hold values from 0 to 127, as said below
- target_place: int32 [10240], P('cells'), may hold values from 0 to 79, as said below
- adjacent_bins: int32 [27, 10240], P(None, 'cells'), may hold values from 0 to 10239, as said below
Outputs:
- new_velocity: float32 [3, 655360], P(None, 'cells')
- density: float32 [655360], P('cells')
Inputs may be any that keep to these rules, and one draw needn't show every extreme that they name: `target_processor`: one device's blocks go to exactly 40 distinct devices, exactly 2 blocks to each; every device receives exactly 80 blocks. The pairs (target_processor, target_place) of all blocks are distinct, so every slot of every device receives one block. `adjacent_bins`: entry 13 of a cell is the cell itself. Every other entry of a cell on device d names a different cell on device d, one of the last 40 cells of device d - 1, or one of the first 40 cells of device d + 1 (global index = device * 80 + slot). Entries may repeat. `alive_tally`: 64 is reached.
All inputs are finite; a program needn't handle non-finite values.
Results may differ from a plain program's by a relative error of at most 0.00013.
Values sent between devices are 32-bit elements; how exact they have to be, the bound alone decides.
No kernel may reach another device: no remote copies, remote signals or barrier semaphores. Data moves between devices by JAX's collectives and lax.ppermute only.
A program may use at most 64 MiB of HBM per device.

v0:
```python
import jax
import jax.numpy as jnp
from jax import lax
from jax.sharding import PartitionSpec as P

BIN_PLACES = 64
NEIGH = 27


step_time = 0.5
mass_rate = 0.3
visc_scale = 0.01
dens_scale = 0.01
heat_slope = 3.0
jamming_bound = 0.6
centre_entry = 13
field_count = 9
entries_per_turn = 3


def extended_2(cells, sides, width):
    for axis, dim in sides:
        count = lax.axis_size(axis)
        ends = count - 1
        head = lax.slice_in_dim(cells, 0, width, axis=dim)
        tail = lax.slice_in_dim(cells, cells.shape[dim] - width, cells.shape[dim], axis=dim)
        cells = jnp.concatenate(
            [
                lax.ppermute(tail, axis, [(i, (i + 1) % count) for i in range(ends)]),
                cells,
                lax.ppermute(head, axis, [((i + 1) % count, i) for i in range(ends)]),
            ],
            axis=dim,
        )
    return cells


def stiffness_of_heat(scaled_heat, solid_share):
    return jnp.exp(-heat_slope * scaled_heat) * (1.0 - solid_share / jamming_bound) ** (-2.5)


def base_weights(own_pos, other_pos):
    dist_sq = (own_pos[:, 0, :, None] - other_pos[:, 0, None, :]) ** 2
    dist_sq = dist_sq + (own_pos[:, 1, :, None] - other_pos[:, 1, None, :]) ** 2
    dist_sq = dist_sq + (own_pos[:, 2, :, None] - other_pos[:, 2, None, :]) ** 2
    return jnp.maximum(1.0 - dist_sq, 0.0)


def density_turn(own_pos, source_pos, source_mass):

    def advance(entry_index, index_row, carried):
        other_pos = jnp.take(source_pos, index_row, axis=0)
        other_mass = jnp.take(source_mass, index_row, axis=0)
        weight = base_weights(own_pos, other_pos)
        return carried + jnp.sum(weight * weight * weight * other_mass[:, None, :], axis=2)

    return advance


def viscous_turn(own_pos, own_visc, source_pos, source_visc, source_coef, source_vel):
    off_diagonal = 1.0 - jnp.eye(BIN_PLACES, dtype=jnp.float32)

    def advance(entry_index, index_row, carried):
        numer, denom = carried
        other_pos = jnp.take(source_pos, index_row, axis=0)
        other_visc = jnp.take(source_visc, index_row, axis=0)
        other_coef = jnp.take(source_coef, index_row, axis=0)
        other_vel = jnp.take(source_vel, index_row, axis=0)
        weight = base_weights(own_pos, other_pos)
        mean_visc = (
            2.0
            * own_visc[:, :, None]
            * other_visc[:, None, :]
            / (own_visc[:, :, None] + other_visc[:, None, :])
        )
        couple = mean_visc * weight * weight * other_coef[:, None, :]
        couple = jnp.where(entry_index == centre_entry, couple * off_diagonal, couple)
        numer = numer + jnp.einsum(
            "bij,bcj->bci", couple, other_vel, precision=lax.Precision.HIGHEST
        )
        denom = denom + jnp.sum(couple, axis=2)
        return (numer, denom)

    return advance


def finish(numer, denom, rate_mass, own_vstar, live):
    total_diag = rate_mass + denom
    safe_diag = jnp.where(live > 0, total_diag, 1.0)
    value = (rate_mass[:, None, :] * own_vstar + numer) / safe_diag[:, None, :]
    return jnp.where(live[:, None, :] > 0, value, 0.0)


def over_entries(local_index, advance, start_value):
    group_total = NEIGH // entries_per_turn

    def loop_body(group_index, carried):
        for inner in range(entries_per_turn):
            entry_index = group_index * entries_per_turn + inner
            index_row = lax.dynamic_index_in_dim(local_index, entry_index, 0, keepdims=False)
            carried = advance(entry_index, index_row, carried)
        return carried

    return lax.fori_loop(0, group_total, loop_body, start_value)


def scatter_rows(target, values, buffer_rows, fill_value):
    base = jnp.full((buffer_rows,) + values.shape[1:], fill_value, values.dtype)
    return base.at[target].set(values, mode="drop")


def place_rows(values, slot_value, length):
    position = slot_value.astype(jnp.int32)
    valid = (slot_value >= 0) & (position >= 0) & (position < length)
    position = jnp.where(valid, position, length)
    base = jnp.zeros((length,) + values.shape[1:], values.dtype)
    return base.at[position].set(values, mode="drop")


def body(
    parcel_locations,
    parcel_speed,
    explicit_forcing,
    parcel_weight,
    scaled_heat,
    solid_share,
    alive_tally,
    target_processor,
    target_place,
    adjacent_bins,
):
    devices = lax.axis_size("cells")
    device_rank = lax.axis_index("cells")
    bin_lattice = alive_tally.shape[0]
    capacity = max(2, 2 * bin_lattice // devices)
    rim_cells = bin_lattice // 2
    row_width = field_count * BIN_PLACES
    slot_iota = lax.broadcasted_iota(jnp.int32, (bin_lattice, BIN_PLACES), 1)
    live_before = (slot_iota < alive_tally[:, None]).astype(jnp.float32)
    trial_speed_vector = parcel_speed + step_time * explicit_forcing
    hidden_entries = parcel_weight.reshape(bin_lattice, BIN_PLACES) * live_before
    quantity_stack = jnp.concatenate(
        [
            parcel_locations.reshape(3, bin_lattice, BIN_PLACES),
            trial_speed_vector.reshape(3, bin_lattice, BIN_PLACES),
            hidden_entries[None],
            scaled_heat.reshape(1, bin_lattice, BIN_PLACES),
            solid_share.reshape(1, bin_lattice, BIN_PLACES),
        ],
        0,
    )
    payload = jnp.transpose(quantity_stack, (1, 0, 2)).reshape(bin_lattice, row_width)
    peer_iota = lax.broadcasted_iota(jnp.int32, (bin_lattice, devices), 1)
    onehot = (target_processor[:, None] == peer_iota).astype(jnp.int32)
    earlier = jnp.cumsum(onehot, axis=0) - onehot
    place_in_peer = jnp.sum(earlier * onehot, axis=1)
    slot_value = target_place.astype(jnp.float32)
    count_value = alive_tally.astype(jnp.float32)
    buffer_rows = devices * capacity
    target = target_processor * capacity + place_in_peer
    sent_rows = scatter_rows(target, payload, buffer_rows, 0.0).reshape(
        devices, capacity, row_width
    )
    sent_slot = scatter_rows(target, slot_value, buffer_rows, -1.0).reshape(devices, capacity)
    sent_count = scatter_rows(target, count_value, buffer_rows, 0.0).reshape(devices, capacity)
    got_rows, got_slot, got_count = (
        lax.all_to_all(sent_rows, "cells", split_axis=0, concat_axis=0, tiled=True),
        lax.all_to_all(sent_slot, "cells", split_axis=0, concat_axis=0, tiled=True),
        lax.all_to_all(sent_count, "cells", split_axis=0, concat_axis=0, tiled=True),
    )
    flat_slot = got_slot.reshape(-1)
    own_state = place_rows(got_rows.reshape(-1, row_width), flat_slot, bin_lattice)
    own_count = place_rows(got_count.reshape(-1), flat_slot, bin_lattice)
    extended = extended_2(own_state, (("cells", 0),), rim_cells)
    bin_groups = extended.reshape(bin_lattice + 2 * rim_cells, field_count, BIN_PLACES)
    ext_pos = bin_groups[:, 0:3]
    ext_vstar = bin_groups[:, 3:6]
    ext_mass = bin_groups[:, 6]
    widened_stiffness = stiffness_of_heat(bin_groups[:, 7], bin_groups[:, 8])
    own_pos = ext_pos[rim_cells : rim_cells + bin_lattice]
    own_vstar = ext_vstar[rim_cells : rim_cells + bin_lattice]
    own_mass = ext_mass[rim_cells : rim_cells + bin_lattice]
    own_visc = widened_stiffness[rim_cells : rim_cells + bin_lattice]
    live = (slot_iota < own_count.astype(jnp.int32)[:, None]).astype(jnp.float32)
    local_index = adjacent_bins - device_rank * bin_lattice + rim_cells
    density_advance = density_turn(own_pos, ext_pos, ext_mass)
    raw = dens_scale * over_entries(
        local_index, density_advance, jnp.zeros((bin_lattice, BIN_PLACES), jnp.float32)
    )
    safe_own = jnp.where(live > 0, raw, 1.0)
    density = jnp.where(live > 0, raw, 0.0)
    ext_safe = extended_2(safe_own, (("cells", 0),), rim_cells)
    ext_coef = visc_scale * ext_mass / ext_safe
    rate_mass = mass_rate * own_mass

    def sweep(ext_vel):
        viscous_advance = viscous_turn(
            own_pos, own_visc, ext_pos, widened_stiffness, ext_coef, ext_vel
        )
        start_value = (
            jnp.zeros((bin_lattice, 3, BIN_PLACES), jnp.float32),
            jnp.zeros((bin_lattice, BIN_PLACES), jnp.float32),
        )
        numer, denom = over_entries(local_index, viscous_advance, start_value)
        return finish(numer, denom, rate_mass, own_vstar, live)

    first_sweep = sweep(ext_vstar)
    ext_first = extended_2(
        first_sweep.reshape(bin_lattice, 3 * BIN_PLACES), (("cells", 0),), rim_cells
    )
    second_sweep = sweep(ext_first.reshape(bin_lattice + 2 * rim_cells, 3, BIN_PLACES))
    new_velocity = jnp.transpose(second_sweep, (1, 0, 2)).reshape(3, bin_lattice * BIN_PLACES)
    return (new_velocity, density.reshape(bin_lattice * BIN_PLACES))


def solution(mesh):
    placed = (
        P(None, "cells"),
        P(None, "cells"),
        P(None, "cells"),
        P("cells"),
        P("cells"),
        P("cells"),
        P("cells"),
        P("cells"),
        P("cells"),
        P(None, "cells"),
    )
    return jax.shard_map(
        body, mesh=mesh, in_specs=placed, out_specs=(P(None, "cells"), P("cells")), check_vma=False
    )
```

profile of v0, /device:TPU:121, one launch (start us, length us, event | category | flops | bytes accessed | tf_op | source)
XLA Modules:
  0.0 1013.2 jit_solution(3160298085241603887)
XLA Ops:
  5.3 10.0 all-to-all-start
  20.4 9.0 all-to-all-start.1
  34.5 9.0 all-to-all-start.2
  73.5 82.5 %while.54 = (s32[]{:T(128)}, f32[80,64]{0,1:T(8,128)S(1)}, f32[80,3,64]{0,2,1:T(8,128)S(1)}, s32[27,80]{1,0:T(8,128)S(1)}, f32[160,3,64]{2,1,0:T(4,128)S(1)}, /*...) while((s32[]{:T(128)}, f32[80,64]{0,1:T(8,128)S(1)}, ...), condition=%wide.region_11.14_spmd.clone, body=%wide.region_7.13_spmd.clone.sunk | while | flops 13833647 | bytes 2455213 | solution.py:104
  167.7 415.8 %while.55 = (s32[]{:T(128)}, f32[80,3,64]{2,1,0:T(4,128)S(1)}, f32[80,64]{1,0:T(8,128)S(1)}, s32[27,80]{1,0:T(8,128)S(1)}, f32[160,3,64]{2,1,0:T(4,128)S(1)}, /*...) while((s32[]{:T(128)}, f32[80,3,64]{2,1,0:T(4,128)S(1)}, ...), condition=%wide.region_16.19_spmd.clone.clone, body=%wide.region_12.18_spmd.clone.clone.sunk | while | flops 71973296 | bytes 4091751 | solution.py:104
  187.2 8.4 fusion.154
  196.3 8.4 fusion.152
  205.4 8.5 fusion.156
  233.4 8.4 fusion.154
  242.5 8.4 fusion.152
  251.6 8.5 fusion.156
  279.6 8.4 fusion.154
  288.7 8.4 fusion.152
  297.8 8.5 fusion.156
  325.8 8.4 fusion.154
  334.9 8.4 fusion.152
  344.0 8.5 fusion.156
  372.0 8.4 fusion.154
  381.1 8.4 fusion.152
  390.2 8.5 fusion.156
  427.3 8.4 fusion.152
  436.4 8.5 fusion.156
  464.4 8.4 fusion.154
  473.5 8.4 fusion.152
  482.6 8.5 fusion.156
  519.7 8.4 fusion.152
  528.8 8.5 fusion.156
  565.9 8.4 fusion.152
  575.0 8.5 fusion.156
  596.1 415.8 %while.56 = (s32[]{:T(128)}, f32[80,3,64]{2,1,0:T(4,128)S(1)}, f32[80,64]{1,0:T(8,128)S(1)}, s32[27,80]{1,0:T(8,128)S(1)}, f32[160,3,64]{2,1,0:T(4,128)S(1)}, /*...) while((s32[]{:T(128)}, f32[80,3,64]{2,1,0:T(4,128)S(1)}, ...), condition=%wide.region_21.24_spmd.clone.clone, body=%wide.region_17.23_spmd.clone.clone.sunk | while | flops 71973296 | bytes 4091751 | solution.py:104
  624.7 8.4 fusion.164
  633.8 8.5 fusion.168
  670.9 8.4 fusion.164
  680.0 8.5 fusion.168
  717.1 8.4 fusion.164
  726.2 8.5 fusion.168
  763.3 8.4 fusion.164
  772.4 8.5 fusion.168
  809.5 8.4 fusion.164
  818.6 8.5 fusion.168
  855.7 8.4 fusion.164
  864.8 8.5 fusion.168
  901.9 8.4 fusion.164
  911.0 8.5 fusion.168
  948.1 8.4 fusion.164
  957.2 8.5 fusion.168
  994.3 8.4 fusion.164
  1003.4 8.5 fusion.168
  (914 shorter events, 623.7 us)
Async XLA Ops:
  0.6 15.8 %copy-start = (f32[3,5120]{1,0:T(4,128)S(1)}, f32[3,5120]{1,0:T(4,128)}, u32[]{:S(2)}) copy-start(f32[3,5120]{1,0:T(4,128)} %param.21) | copy-start | bytes 184324
  0.6 15.8 %copy-start.1 = (f32[3,5120]{1,0:T(4,128)S(1)}, f32[3,5120]{1,0:T(4,128)}, u32[]{:S(2)}) copy-start(f32[3,5120]{1,0:T(4,128)} %param.22) | copy-start | bytes 184324
  0.7 15.9 %copy-start.2 = (f32[5120]{0:T(1024)S(1)}, f32[5120]{0:T(1024)}, u32[]{:S(2)}) copy-start(f32[5120]{0:T(1024)} %param.23) | copy-start | bytes 61444
  1.4 15.2 %copy-start.3 = (f32[5120]{0:T(1024)S(1)}, f32[5120]{0:T(1024)}, u32[]{:S(2)}) copy-start(f32[5120]{0:T(1024)} %param.24) | copy-start | bytes 61444
  5.3 15.1 %all-to-all-start = ((f32[128,1,2]{2,1,0:T(1,128)}), f32[128,1,2]{2,1,0:T(1,128)S(1)}, u32[]{:S(2)}, u32[]{:S(2)}) async-start(f32[128,1,2]{2,1,0:T(1,128)} %bitcast), calls=%async_computation | async-start | bytes 131072 | tf_op jit(solution)/shard_map/all_to_all | solution.py:168
  15.4 1.4 copy-start.6
  16.4 0.7 copy-start.4
  20.4 14.1 %all-to-all-start.1 = ((f32[128,1,2]{2,1,0:T(1,128)}), f32[128,1,2]{2,1,0:T(1,128)S(1)}, u32[]{:S(2)}, u32[]{:S(2)}) async-start(f32[128,1,2]{2,1,0:T(1,128)} %bitcast.2), calls=%async_computation.1 | async-start | bytes 131072 | tf_op jit(solution)/shard_map/all_to_all | solution.py:169
  32.0 11.5 %copy-start.5 = (s32[27,80]{1,0:T(8,128)S(1)}, s32[27,80]{1,0:T(8,128)}, u32[]{:S(2)}) copy-start(s32[27,80]{1,0:T(8,128)} %param.29) | copy-start | bytes 25924
  34.5 19.4 %all-to-all-start.2 = ((f32[128,2,576]{2,1,0:T(2,128)}), f32[128,2,576]{2,1,0:T(2,128)S(1)}, u32[]{:S(2)}, u32[]{:S(2)}) async-start(f32[128,2,576]{2,1,0:T(2,128)} %reshape.234), calls=%async_computation.2 | async-start | bytes 1310720 | tf_op jit(solution)/shard_map/all_to_all | solution.py:167
  55.8 8.6 collective-permute-start
  62.5 10.2 %collective-permute-start.1 = (f32[40,576]{1,0:T(8,128)S(1)}, f32[40,576]{1,0:T(8,128)S(1)}, u32[]{:S(2)}, u32[]{:S(2)}) collective-permute-start(f32[40,576]{1,0:T(8,128)S(1)} %get-tuple-element.1139), channel_id=1, source_target_pairs={{1,0},{2,1},{3,2},{4,3},{5,4},{6,5},{7,6},{8,7},{9,8},{10,9},{11,1... | collective-permute-start | bytes 276488 | tf_op jit(solution)/shard_map/ppermute | solution.py:31
  156.1 5.1 collective-permute-start.2
  158.0 9.5 collective-permute-start.3
  584.1 5.4 collective-permute-start.4
  586.1 9.5 collective-permute-start.5
where the time goes:
time: 1010 us
  matrix products  456 us (45%)
  other arithmetic  268 us (27%)
  local copies, waits for them, and re-layouts  206 us (20%)
  starting transfers between devices  45.7 us (5%)
  waiting for transfers between devices  31.4 us (3%)
    dot_general x54, matrix products, advance(): jnp.einsum('bij,bcj->bci', couple, other_vel, precision=lax.Precision.HIG...  456 us
    reduce_sum x36, other arithmetic, advance(): denom = denom + jnp.sum(couple, axis=2)  216 us
    gather x81, local copies, waits for them, and re-layouts, advance(): other_pos = jnp.take(source_pos, index_row, axis=0)  55.2 us
    gather x54, local copies, waits for them, and re-layouts, advance(): other_vel = jnp.take(source_vel, index_row, axis=0)  37.1 us
    gather x54, local copies, waits for them, and re-layouts, advance(): other_visc = jnp.take(source_visc, index_row, axis=0)  32.9 us
    gather x54, local copies, waits for them, and re-layouts, advance(): other_coef = jnp.take(source_coef, index_row, axis=0)  32.8 us
    reduce_sum x9, other arithmetic, advance(): jnp.sum(weight * weight * weight * other_mass[:, None, :], axis=2)  29.4 us
    ppermute x3, waiting for transfers between devices, extended_2(): lax.ppermute(head, axis, [((i + 1) % count, i) for i in range(ends)])  20.5 us
  transfers between devices with their start and end apart: 9, of which 6 were waited for; matrix products, arithmetic and copies ran while one was open for 1% of the time, Pallas kernels for 0%

commit v1 on v0

v1 whole, which is shorter than its diff:
```python
import functools

import jax
import jax.numpy as jnp
from jax import lax
from jax.experimental import pallas as pl
from jax.experimental.pallas import tpu as pltpu
from jax.sharding import PartitionSpec as P

SLOTS = 64
NEIGH = 27
ENTRY_ORDER = (13,) + tuple(range(13)) + tuple(range(14, 27))
ROWS = 14
WIDTH = ROWS * 128
CHUNK = 32
GROUP = 8
FIELDS = 8
PEER_ROWS = FIELDS + 1
TERMS = 32

step_time = 0.5
mass_rate = 0.3
visc_scale = 0.01
dens_scale = 0.01
heat_slope = 3.0
jamming_bound = 0.6

VMEM = pltpu.MemorySpace.VMEM
SMEM = pltpu.MemorySpace.SMEM
HBM = pltpu.MemorySpace.HBM
MIB = 1 << 20
BF16 = jnp.bfloat16
F32 = jnp.float32


def lane_iota(shape):
    return lax.broadcasted_iota(jnp.int32, shape, len(shape) - 1)


def sub_iota(shape):
    return lax.broadcasted_iota(jnp.int32, shape, len(shape) - 2)


def split_bf16(value, count):
    parts = []
    for _ in range(count):
        part = value.astype(BF16).astype(F32)
        parts.append(part)
        value = value - part
    return parts


def pack_kernel(*refs):
    inputs, sent, local, out, fields, seen, sems, out_sem = refs[:9], refs[9], refs[10:19], *refs[19:]
    copies = [pltpu.make_async_copy(a, b, sems.at[i]) for i, (a, b) in enumerate(zip(inputs, local))]
    for copy in copies:
        copy.start()
    tally, peer, place, pos, speed, force, weight, heat, share = local
    cells = tally.shape[0]
    peers = out.shape[0] // PEER_ROWS
    lane = lane_iota((1, 128))
    low = lane < SLOTS

    def clear(index, carry):
        seen[index] = 0
        out[pl.ds(index * PEER_ROWS + FIELDS, 1), :] = jnp.full((1, 128), -1.0, F32)
        return carry

    lax.fori_loop(0, peers, clear, 0, unroll=8)
    for copy in copies:
        copy.wait()
    open_bound = 1.0 - share[...] / jamming_bound
    resist = jnp.exp(heat_slope * heat[...]) * (open_bound * open_bound * jnp.sqrt(open_bound))
    for pair in range(cells // 2):
        span = pl.ds(pair * 128, 128)
        bound = jnp.where(low, tally[2 * pair], tally[2 * pair + 1] + SLOTS)
        live = (lane < bound).astype(F32)
        fields[pair, 0:3, :] = pos[:, span]
        fields[pair, 3:6, :] = speed[:, span] + step_time * force[:, span]
        fields[pair, 6:7, :] = weight[pair : pair + 1, :] * live
        fields[pair, 7:8, :] = resist[pair : pair + 1, :]
    half_of = lane_iota((FIELDS, 128)) // SLOTS

    def send(pair, carry):
        tile = fields[pair]
        turned = pltpu.roll(tile, SLOTS, 1)
        for side in range(2):
            cell = 2 * pair + side
            target = peer[cell]
            half = seen[target]
            seen[target] = 1
            row = target * PEER_ROWS
            value = jnp.where(half == side, tile, turned)
            pltpu.store(out.at[pl.ds(row, FIELDS), :], value, mask=half_of == half)
            first = half * SLOTS
            head = jnp.where(lane == first, place[cell].astype(F32), tally[cell].astype(F32))
            pltpu.store(
                out.at[pl.ds(row + FIELDS, 1), :], head, mask=(lane == first) | (lane == first + 1)
            )
        return carry

    lax.fori_loop(0, cells // 2, send, 0, unroll=4)
    copy = pltpu.make_async_copy(out, sent, out_sem)
    copy.start()
    copy.wait()


def unpack_kernel(got, head, tail, count, heads_v, heads_s, store, sem):
    peers = got.shape[0] // PEER_ROWS
    pairs = store.shape[0] - 1
    heads = jnp.transpose(got[pl.ds(FIELDS, peers, stride=PEER_ROWS), :])
    heads_v[0:2, :] = heads[0:2].astype(jnp.int32)
    heads_v[2:4, :] = heads[SLOTS : SLOTS + 2].astype(jnp.int32)
    copy = pltpu.make_async_copy(heads_v, heads_s, sem)
    copy.start()
    copy.wait()
    half_of = lane_iota((FIELDS, 128)) // SLOTS

    def take(source, carry):
        tile = got[pl.ds(source * PEER_ROWS, FIELDS), :]
        turned = pltpu.roll(tile, SLOTS, 1)
        for half in range(2):
            slot = heads_s[2 * half, source]
            slot = jnp.where(slot < 0, 2 * pairs, slot)
            count[slot] = heads_s[2 * half + 1, source]
            side = lax.rem(slot, 2)
            value = jnp.where(side == half, tile, turned)
            pltpu.store(store.at[slot // 2], value, mask=half_of == side)
        return carry

    lax.fori_loop(0, peers, take, 0, unroll=8)
    head[...] = store[0 : pairs // 2]
    tail[...] = store[pairs // 2 : pairs]


def two_halves(tile, low):
    turned = pltpu.roll(tile, SLOTS, 1)
    return (tile, turned), low


def put_halves(tile, low, first, second, index):
    turned = pltpu.roll(tile, SLOTS, 1)
    zero = jnp.zeros_like(tile)
    first[index] = jnp.where(low, tile, zero).astype(first.dtype)
    second[index] = jnp.where(low, zero, turned).astype(first.dtype)
    first[index + 1] = jnp.where(low, turned, zero).astype(first.dtype)
    second[index + 1] = jnp.where(low, zero, tile).astype(first.dtype)


def entries(adj, base, cell, dummy):
    return [adj[n, cell] - base for n in ENTRY_ORDER] + [dummy]


def density_kernel(
    base_ref, adj, count, left, head, tail, right, hi, lo, dens, coef_head, coef_tail,
    terms_a, terms_b, ext, stage, lhs, own_r, rows_t, rows_f, acc, raw,
):
    rim = 2 * head.shape[0]
    quarter = head.shape[0]
    dummy = 4 * rim
    base = base_ref[0]
    step = pl.program_id(0)
    low8 = lane_iota((FIELDS, 128)) < SLOTS
    low32 = lane_iota((TERMS, 128)) < SLOTS
    sub8 = sub_iota((FIELDS, 128))

    @pl.when(step == 0)
    def _():
        ext[dummy] = jnp.where(sub8 == 7, 1.0, 0.0)
        terms_a[dummy] = jnp.zeros((TERMS, 128), BF16)
        terms_b[dummy] = jnp.zeros((TERMS, 128), BF16)
        ones = jnp.where(sub8 < 3, 1.0, 0.0)
        for part, ref in enumerate((left, head, tail, right)):
            for pair in range(quarter):
                tile = ref[pair]
                slot = part * rim + 2 * pair
                turned = pltpu.roll(tile, SLOTS, 1)
                ext[slot] = jnp.where(low8, tile, turned)
                ext[slot + 1] = jnp.where(low8, turned, tile)
                x, y, z = tile[0:1], tile[1:2], tile[2:3]
                length = x * x + y * y + z * z
                vector = jnp.where(sub8 == 3, -length, tile)
                v1, v2, v3 = split_bf16(vector, 3)
                at = slot // 2 % 8
                for row, v in enumerate((v1, v2, v3, v1, v2, v1)):
                    stage[at, 4 * row : 4 * row + 4, :] = v[0:4]
                stage[at, 24:32, :] = ones
                put_halves(stage[at], low32, terms_a, terms_b, slot)
                if part in (1, 2):
                    own = (part - 1) * quarter + pair
                    vector = jnp.where(sub8 == 3, 1.0, 2.0 * tile)
                    w1, w2, w3 = split_bf16(vector, 3)
                    a1, a2, a3 = split_bf16(1.0 - length, 3)
                    at = 8 + pair % 8
                    for row, w in enumerate((w1, w1, w1, w2, w2, w3)):
                        stage[at, 4 * row : 4 * row + 4, :] = w[0:4]
                    extra = jnp.where(sub8 == 0, a1, jnp.where(sub8 == 1, a2, a3))
                    stage[at, 24:32, :] = jnp.where(sub8 < 3, extra, tile[7:8])
                    turned = jnp.transpose(stage[at])
                    lhs[own] = turned.astype(BF16)
                    own_r[own] = jnp.broadcast_to(turned[:, 31:32], (128, 128))

    chunk_lane = lane_iota((CHUNK, 128))
    chunk_sub = sub_iota((CHUNK, 128))

    def one_cell(local, carry):
        cell = step * GROUP + local
        index = entries(adj, base, cell, dummy)
        for p in range(ROWS):
            i, j = index[2 * p], index[2 * p + 1]
            rows_f[p] = jnp.where(low8, ext[i], ext[j])
            rows_t[:, p * 128 : p * 128 + 128] = terms_a[i] + terms_b[j]

        def turn(part, carry):
            first = pl.multiple_of(part * CHUNK, CHUNK)
            place = pl.multiple_of(lax.rem(cell, 2) * SLOTS + first, CHUNK)
            own = lhs[cell // 2, pl.ds(place, CHUNK), :]
            ri = own_r[cell // 2, pl.ds(place, CHUNK), :]
            total = jnp.zeros((CHUNK, 128), F32)
            for p2 in range(ROWS // 2):
                wide = jnp.dot(
                    own, rows_t[:, p2 * 256 : p2 * 256 + 256], preferred_element_type=F32
                )
                for p in (2 * p2, 2 * p2 + 1):
                    q = jnp.maximum(wide[:, (p % 2) * 128 : (p % 2) * 128 + 128], 0.0)
                    q2 = q * q
                    total = total + q2 * (q * rows_f[p, 6:7, :])
                    value = q2 * pl.reciprocal(ri + rows_f[p, 7:8, :])
                    if p == 0:
                        value = jnp.where(chunk_lane == chunk_sub + first, 0.0, value)
                    upper = value.astype(BF16)
                    span = slice(p * 128, p * 128 + 128)
                    hi[local, pl.ds(first, CHUNK), span] = upper
                    lo[local, pl.ds(first, CHUNK), span] = (value - upper.astype(F32)).astype(BF16)
            acc[cell, pl.ds(first, CHUNK), :] = total
            return carry

        return lax.fori_loop(0, (count[cell] + CHUNK - 1) // CHUNK, turn, carry)

    lax.fori_loop(0, GROUP, one_cell, 0)

    @pl.when(step == pl.num_programs(0) - 1)
    def _():
        ones = jnp.ones((FIELDS, 128), BF16)

        def reduce_pair(pair, carry):
            total = jnp.zeros((FIELDS, 128), F32)
            for part in split_bf16(acc[pl.ds(2 * pair, 2)].reshape(2 * SLOTS, 128), 3):
                total = total + lax.dot_general(
                    ones, part.astype(BF16), (((1,), (1,)), ((), ())), preferred_element_type=F32
                )
            raw[pl.ds(pair, 1), :] = total[0:1]
            return carry

        lax.fori_loop(0, 2 * quarter, reduce_pair, 0, unroll=4)
        for part, (ref, coef) in enumerate(((head, coef_head), (tail, coef_tail))):
            mass = ref[:, 6, :]
            live = mass > 0.0
            value = dens_scale * raw[part * quarter : (part + 1) * quarter, :]
            dens[part * quarter : (part + 1) * quarter, :] = jnp.where(live, value, 0.0)
            coef[...] = (2.0 * visc_scale) * mass / jnp.where(live, value, 1.0)


def sweep_kernel(is_first, base_ref, adj, hi, lo, *refs):
    coefs, speeds, refs = refs[:4], refs[4:8], refs[8:]
    if is_first:
        (head, tail), (out_head, out_tail), refs = speeds[1:3], refs[:2], refs[2:]
    else:
        (head, tail), (out,), refs = refs[:2], refs[2:3], refs[3:]
    ext_a, ext_b, rows, sums, stage = refs
    quarter = head.shape[0]
    rim = 2 * quarter
    dummy = 4 * rim
    base = base_ref[0]
    step = pl.program_id(0)
    low = lane_iota((FIELDS, 128)) < SLOTS
    low16 = lane_iota((2 * FIELDS, 128)) < SLOTS
    sub = sub_iota((FIELDS, 128))
    moving = (sub >= 3) & (sub < 6)

    @pl.when(step == 0)
    def _():
        ext_a[dummy] = jnp.zeros((2 * FIELDS, 128), BF16)
        ext_b[dummy] = jnp.zeros((2 * FIELDS, 128), BF16)
        for part in range(4):
            for pair in range(quarter):
                tile = jnp.where(sub == 0, 1.0, jnp.where(moving, speeds[part][pair], 0.0))
                w1, w2 = split_bf16(tile * coefs[part][pair : pair + 1, :], 2)
                at = pair % 8
                stage[at, 0:FIELDS, :] = w1
                stage[at, FIELDS:, :] = w2
                put_halves(stage[at], low16, ext_a, ext_b, part * rim + 2 * pair)

    def one_cell(local, carry):
        cell = step * GROUP + local
        index = entries(adj, base, cell, dummy)
        at = lax.rem(local, 4)
        for p in range(ROWS):
            rows[at, :, p * 128 : p * 128 + 128] = ext_a[index[2 * p]] + ext_b[index[2 * p + 1]]
        total = jnp.zeros((2 * FIELDS, SLOTS), F32)
        for part in (hi, lo):
            total = total + lax.dot_general(
                rows[at], part[local], (((1,), (1,)), ((), ())), preferred_element_type=F32
            )
        sums[cell, :, 0:SLOTS] = total[0:FIELDS] + total[FIELDS:]
        return carry

    lax.fori_loop(0, GROUP, one_cell, 0, unroll=4)

    @pl.when(step == pl.num_programs(0) - 1)
    def _():
        for part, ref in enumerate((head, tail)):
            for pair in range(quarter):
                slot = part * quarter + pair
                tile = ref[pair]
                total = jnp.where(low, sums[2 * slot], pltpu.roll(sums[2 * slot + 1], SLOTS, 1))
                live = jnp.broadcast_to(tile[6:7] > 0.0, (FIELDS, 128))
                rate = mass_rate * tile[6:7]
                below = jnp.broadcast_to(rate + total[0:1], (FIELDS, 128))
                value = (rate * tile + total) / jnp.where(live, below, 1.0)
                value = jnp.where(live & moving, value, 0.0)
                if is_first:
                    (out_head, out_tail)[part][pair] = value
                else:
                    out[:, slot * 128 : slot * 128 + 128] = value[3:6]


def call(kernel, outs, scratch, in_specs, args, out_specs=None, grid=None, vmem=40):
    extra = {} if grid is None else {"grid": grid}
    return pl.pallas_call(
        kernel,
        out_shape=outs,
        in_specs=in_specs,
        out_specs=out_specs,
        scratch_shapes=scratch,
        compiler_params=pltpu.CompilerParams(vmem_limit_bytes=vmem * MIB),
        **extra,
    )(*args)


def f32(*shape):
    return jax.ShapeDtypeStruct(shape, F32)


def spec(space):
    return pl.BlockSpec(memory_space=space)


def whole(*shape):
    return pl.BlockSpec(shape, lambda g: (0,) * len(shape))


def density(base, adj, count, left, head, tail, right):
    quarter = head.shape[0]
    cells, pairs = 4 * quarter, 2 * quarter
    ext = 2 * cells + 1
    tile = whole(quarter, FIELDS, 128)
    block = pl.BlockSpec((GROUP, SLOTS, WIDTH), lambda g: (g, 0, 0))
    return call(
        density_kernel,
        [jax.ShapeDtypeStruct((cells, SLOTS, WIDTH), BF16)] * 2
        + [f32(pairs, 128), f32(quarter, 128), f32(quarter, 128)],
        [pltpu.VMEM((ext, TERMS, 128), BF16)] * 2
        + [
            pltpu.VMEM((ext, FIELDS, 128), F32),
            pltpu.VMEM((16, TERMS, 128), F32),
            pltpu.VMEM((pairs, 128, TERMS), BF16),
            pltpu.VMEM((pairs, 128, 128), F32),
            pltpu.VMEM((TERMS, WIDTH), BF16),
            pltpu.VMEM((ROWS, FIELDS, 128), F32),
            pltpu.VMEM((cells, SLOTS, 128), F32),
            pltpu.VMEM((pairs, 128), F32),
        ],
        [spec(SMEM)] * 3 + [tile] * 4,
        (base, adj, count, left, head, tail, right),
        out_specs=[block] * 2 + [whole(pairs, 128), whole(quarter, 128), whole(quarter, 128)],
        grid=(cells // GROUP,),
    )


def sweep(is_first, base, adj, hi, lo, coefs, speeds, head, tail):
    quarter = head.shape[0]
    cells = 4 * quarter
    ext = 2 * cells + 1
    tile = whole(quarter, FIELDS, 128)
    block = pl.BlockSpec((GROUP, SLOTS, WIDTH), lambda g: (g, 0, 0))
    own = () if is_first else (head, tail)
    if is_first:
        outs, out_specs = [f32(quarter, FIELDS, 128)] * 2, [tile] * 2
    else:
        outs, out_specs = [f32(3, cells * SLOTS)], [whole(3, cells * SLOTS)]
    return call(
        functools.partial(sweep_kernel, is_first),
        outs,
        [pltpu.VMEM((ext, 2 * FIELDS, 128), BF16)] * 2
        + [
            pltpu.VMEM((4, 2 * FIELDS, WIDTH), BF16),
            pltpu.VMEM((cells, FIELDS, 128), F32),
            pltpu.VMEM((8, 2 * FIELDS, 128), F32),
        ],
        [spec(SMEM)] * 2 + [block] * 2 + [whole(quarter, 128)] * 4 + [tile] * (4 + len(own)),
        (base, adj, hi, lo) + tuple(coefs) + tuple(speeds) + own,
        out_specs=out_specs,
        grid=(cells // GROUP,),
    )


def body(pos, speed, force, weight, heat, share, tally, peer, place, adj):
    peers = lax.axis_size("cells")
    rank = lax.axis_index("cells")
    cells = tally.shape[0]
    rim = cells // 2
    quarter = cells // 4
    pairs = cells // 2
    right_going = [(i, i + 1) for i in range(peers - 1)]
    left_going = [(i + 1, i) for i in range(peers - 1)]

    def rims(head, tail):
        return lax.ppermute(tail, "cells", right_going), lax.ppermute(head, "cells", left_going)

    args = (tally, peer, place, pos, speed, force)
    args = args + tuple(v.reshape(pairs, 128) for v in (weight, heat, share))
    (sent,) = call(
        pack_kernel,
        [pltpu.HBM((peers * PEER_ROWS, 128), F32)],
        [(pltpu.SMEM if i < 3 else pltpu.VMEM)(v.shape, v.dtype) for i, v in enumerate(args)]
        + [
            pltpu.VMEM((peers * PEER_ROWS, 128), F32),
            pltpu.VMEM((pairs, FIELDS, 128), F32),
            pltpu.SMEM((peers,), jnp.int32),
            pltpu.SemaphoreType.DMA((9,)),
            pltpu.SemaphoreType.DMA,
        ],
        [spec(pl.ANY)] * 9,
        args,
        out_specs=[spec(HBM)],
    )
    got = lax.all_to_all(
        sent.reshape(peers, 1, PEER_ROWS * 128), "cells", split_axis=0, concat_axis=0, tiled=True
    )
    head, tail, count = call(
        unpack_kernel,
        [f32(quarter, FIELDS, 128)] * 2 + [jax.ShapeDtypeStruct((cells + 1,), jnp.int32)],
        [
            pltpu.VMEM((4, 128), jnp.int32),
            pltpu.SMEM((4, 128), jnp.int32),
            pltpu.VMEM((pairs + 1, FIELDS, 128), F32),
            pltpu.SemaphoreType.DMA,
        ],
        [spec(VMEM)],
        (got.reshape(peers * PEER_ROWS, 128),),
        out_specs=[spec(VMEM)] * 2 + [spec(SMEM)],
    )
    left, right = rims(head, tail)
    base = (rank * cells - rim).astype(jnp.int32).reshape(1)
    hi, lo, dens, coef_head, coef_tail = density(base, adj, count, left, head, tail, right)
    coef_left, coef_right = rims(coef_head, coef_tail)
    coefs = (coef_left, coef_head, coef_tail, coef_right)
    first_head, first_tail = sweep(
        True, base, adj, hi, lo, coefs, (left, head, tail, right), head, tail
    )
    first_left, first_right = rims(first_head, first_tail)
    speeds = (first_left, first_head, first_tail, first_right)
    (out,) = sweep(False, base, adj, hi, lo, coefs, speeds, head, tail)
    return out, dens.reshape(cells * SLOTS)


def solution(mesh):
    split, per_column = P("cells"), P(None, "cells")
    return jax.shard_map(
        body,
        mesh=mesh,
        in_specs=(per_column,) * 3 + (split,) * 6 + (per_column,),
        out_specs=(per_column, split),
        check_vma=False,
    )
```

time: 1010 us -> 157 us (0.16)
  matrix products: 456 us -> 0 us
  other arithmetic: 268 us -> 0 us
  local copies, waits for them, and re-layouts: 206 us -> 7.51 us
  Pallas kernels: 0 us -> 88.8 us
  starting transfers between devices: 45.7 us -> 17.2 us
  blocking collectives: 0 us -> 19.7 us
    dot_general x54 -> x0, matrix products: 456 us -> none  [advance(): jnp.einsum('bij,bcj->bci', couple, other_vel, precision=lax.Precision.HIG...]
    reduce_sum x46 -> x0, other arithmetic: 247 us -> none  [the longest x36 216 us: advance(): denom = denom + jnp.sum(couple, axis=2)]
    gather x270 -> x0, local copies, waits for them, and re-layouts: 175 us -> none  [the longest x81 55.2 us: advance(): other_pos = jnp.take(source_pos, index_row, axis=0)]
    pallas_call x0 -> x5, Pallas kernels: none -> 88.8 us  [call(): pl.pallas_call(kernel, out_shape=outs, in_specs=in_specs, out_specs=out_s...]
    all_to_all x3 -> x0, starting transfers between devices: 28.1 us -> none  [the longest x1 10 us: body(): lax.all_to_all(sent_slot, 'cells', split_axis=0, concat_axis=0, tiled=True)]
    all_to_all x0 -> x1, blocking collectives: none -> 19.7 us  [body(): lax.all_to_all(sent.reshape(peers, 1, PEER_ROWS * 128), 'cells', split_ax...]
    select_n x114 -> x0, other arithmetic: 15.8 us -> none  [the longest x54 10.4 us: advance(): other_pos = jnp.take(source_pos, index_row, axis=0)]
    all_to_all x3 -> x0, waiting for transfers between devices: 10.9 us -> none  [the longest x1 6.82 us: body(): lax.all_to_all(sent_rows, 'cells', split_axis=0, concat_axis=0, tiled=True)]
  transfers between devices with their start and end apart: 9 -> 6, of which waited for: 6 -> 3; matrix products, arithmetic and copies ran while one was open for 1% -> 0% of each run, Pallas kernels for 0% -> 0%
where the time goes in v1:
time: 157 us
  Pallas kernels  88.8 us (57%)
  waiting for transfers between devices  22.8 us (15%)
  blocking collectives  19.7 us (13%)
  starting transfers between devices  17.2 us (11%)
  local copies, waits for them, and re-layouts  7.51 us (5%)
    pallas_call x5, Pallas kernels, call(): pl.pallas_call(kernel, out_shape=outs, in_specs=in_specs, out_specs=out_s...  88.8 us
    ppermute x3, waiting for transfers between devices, rims(): lax.ppermute(head, 'cells', left_going)  22.8 us
    all_to_all x1, blocking collectives, body(): lax.all_to_all(sent.reshape(peers, 1, PEER_ROWS * 128), 'cells', split_ax...  19.7 us
    ppermute x3, starting transfers between devices, rims(): lax.ppermute(tail, 'cells', right_going)  10.9 us
    unnamed x20, local copies, waits for them, and re-layouts  7.51 us
    ppermute x3, starting transfers between devices, rims(): lax.ppermute(head, 'cells', left_going)  6.36 us
  transfers between devices with their start and end apart: 6, of which 3 were waited for; matrix products, arithmetic and copies ran while one was open for 0% of the time, Pallas kernels for 0%

profile of v1, /device:TPU:121, one launch (start us, length us, event | category | flops | bytes accessed | tf_op | source)
XLA Modules:
  0.0 156.8 jit_solution(14216563196064085603)
XLA Ops:
  0.6 0.0 copy-start.1
  0.6 0.9 copy-done.1
  1.5 0.0 copy-start.2
  1.5 0.9 copy-done.2
  2.4 0.0 copy-start.3
  2.4 0.9 copy-done.3
  3.3 0.0 copy-start.4
  3.3 0.7 copy-done.4
  4.0 0.0 copy-start.5
  4.0 0.7 copy-done.5
  4.8 0.0 copy-start.6
  4.8 0.7 copy-done.6
  5.5 0.0 copy-start.7
  5.5 0.7 copy-done.7
  6.1 0.0 copy-start.8
  6.1 0.7 copy-done.8
  6.8 0.0 copy-start.9
  6.8 0.7 copy-done.9
  7.4 2.3 %shard_map.113 = f32[1152,128]{1,0:T(8,128)} custom-call(s32[80]{0:T(128)S(1)} %copy-done.7, s32[80]{0:T(128)S(1)} %copy-done.8, s32[80]{0:T(128)S(1)} %copy-done.9, f32[3,5120]{1,0:T(4,128)S(1)} %copy-done.1, f32[3,5120]{1,0:T(4,128)S(1)} %copy-done.2, f32[3,5120]{1,0:T(4,128)S(1)} %copy-done.3, f32[40,128]{1,0:T(8,128)S(1)} %bitcast.8, ...), custom_call_target="tpu_custom_call" | custom-call | tf_op jit(solution)/shard_map/pallas_call | solution.py:330
  9.8 19.7 %all_to_all.5 = f32[128,1,1152]{2,1,0:T(1,128)S(1)} all-to-all(f32[128,1,1152]{2,1,0:T(1,128)} %bitcast.11), channel_id=1, replica_groups=mesh['cells'=128] {'cells'}, dimensions={0} | all-to-all | bytes 1179648 | tf_op jit(solution)/shard_map/all_to_all | solution.py:438
  29.5 3.6 %shard_map.114 = (f32[20,8,128]{2,1,0:T(8,128)S(1)}, f32[20,8,128]{2,1,0:T(8,128)S(1)}, s32[81]{0:T(128)S(1)}) custom-call(f32[1152,128]{1,0:T(8,128)S(1)} %bitcast.7), custom_call_target="tpu_custom_call" | custom-call | tf_op jit(solution)/shard_map/pallas_call | solution.py:330
  33.1 6.7 %collective-permute-start = (f32[20,8,128]{2,1,0:T(8,128)S(1)}, f32[20,8,128]{2,1,0:T(8,128)S(1)}, u32[]{:S(2)}, u32[]{:S(2)}) collective-permute-start(f32[20,8,128]{2,1,0:T(8,128)S(1)} %get-tuple-element.13.tail.refs_6_.refs_9_), channel_id=1, source_target_pairs={{0,1},{1,2},{2,3},{3,4},{4,5},{5,6},{6,7},{7,8},{8,9},{9,10},{10,1... | collective-permute-start | bytes 245768 | tf_op jit(solution)/shard_map/ppermute | solution.py:419
  39.8 1.9 %collective-permute-start.1 = (f32[20,8,128]{2,1,0:T(8,128)S(1)}, f32[20,8,128]{2,1,0:T(8,128)S(1)}, u32[]{:S(2)}, u32[]{:S(2)}) collective-permute-start(f32[20,8,128]{2,1,0:T(8,128)S(1)} %get-tuple-element.14.head.refs_5_.refs_8_), channel_id=1, source_target_pairs={{1,0},{2,1},{3,2},{4,3},{5,4},{6,5},{7,6},{8,7},{9,8},{10,9},{11,1... | collective-permute-start | bytes 245768 | tf_op jit(solution)/shard_map/ppermute | solution.py:419
  41.7 0.0 collective-permute-done.left.refs_4_
  41.7 8.0 %collective-permute-done.1.right.refs_7_ = f32[20,8,128]{2,1,0:T(8,128)S(1)} collective-permute-done((f32[20,8,128]{2,1,0:T(8,128)S(1)}, f32[20,8,128]{2,1,0:T(8,128)S(1)}, u32[]{:S(2)}, u32[]{:S(2)}) %collective-permute-start.1) | collective-permute-done | bytes 81952 | tf_op jit(solution)/shard_map/ppermute | solution.py:419
  49.8 0.0 copy-start
  49.8 0.7 copy-done
  50.5 43.5 %shard_map.115 = (bf16[80,64,1792]{2,1,0:T(8,128)(2,1)}, bf16[80,64,1792]{2,1,0:T(8,128)(2,1)}, f32[40,128]{1,0:T(8,128)}, f32[20,128]{1,0:T(8,128)S(1)}, f32[20,128]{1,0:T(8,128)S(1)}) custom-call(s32[1]{0:T(128)} %bitcast.base_ref, s32[27,80]{1,0:T(8,128)S(1)} %copy-done, s32[81]{0:T(128)S(1)} %get-tuple-element.12.count, ...), custom_call_target="tpu_custom_call" | custom-call | tf_op jit(solution)/shard_map/pallas_call | solution.py:330
  94.0 2.3 %collective-permute-start.2 = (f32[20,128]{1,0:T(8,128)S(1)}, f32[20,128]{1,0:T(8,128)S(1)}, u32[]{:S(2)}, u32[]{:S(2)}) collective-permute-start(f32[20,128]{1,0:T(8,128)S(1)} %get-tuple-element.17.refs_2_), channel_id=1, source_target_pairs={{0,1},{1,2},{2,3},{3,4},{4,5},{5,6},{6,7},{7,8},{8,9},{9,10},{10,1... | collective-permute-start | bytes 30728 | tf_op jit(solution)/shard_map/ppermute | solution.py:419
  96.3 2.0 %collective-permute-start.3 = (f32[20,128]{1,0:T(8,128)S(1)}, f32[20,128]{1,0:T(8,128)S(1)}, u32[]{:S(2)}, u32[]{:S(2)}) collective-permute-start(f32[20,128]{1,0:T(8,128)S(1)} %get-tuple-element.18.refs_1_), channel_id=1, source_target_pairs={{1,0},{2,1},{3,2},{4,3},{5,4},{6,5},{7,6},{8,7},{9,8},{10,9},{11,1... | collective-permute-start | bytes 30728 | tf_op jit(solution)/shard_map/ppermute | solution.py:419
  98.4 0.0 collective-permute-done.2.refs_0_
  98.4 7.2 %collective-permute-done.3.refs_3_ = f32[20,128]{1,0:T(8,128)S(1)} collective-permute-done((f32[20,128]{1,0:T(8,128)S(1)}, f32[20,128]{1,0:T(8,128)S(1)}, u32[]{:S(2)}, u32[]{:S(2)}) %collective-permute-start.3) | collective-permute-done | bytes 10272 | tf_op jit(solution)/shard_map/ppermute | solution.py:419
  105.6 19.3 %shard_map.116 = (f32[20,8,128]{2,1,0:T(8,128)S(1)}, f32[20,8,128]{2,1,0:T(8,128)S(1)}) custom-call(s32[1]{0:T(128)} %bitcast.base_ref, s32[27,80]{1,0:T(8,128)S(1)} %copy-done, bf16[80,64,1792]{2,1,0:T(8,128)(2,1)} %get-tuple-element.15.hi, bf16[80,64,1792]{2,1,0:T(8,128)(2,1)} %get-tuple-element.16.lo, f32[20,128]{1,0:T(8,128)S(1)} %collective-permute-done.2.refs_0_, ...), custom_call_target="tpu_custom_call" | custom-call | tf_op jit(solution)/shard_map/pallas_call | solution.py:330
  124.9 1.9 %collective-permute-start.4 = (f32[20,8,128]{2,1,0:T(8,128)S(1)}, f32[20,8,128]{2,1,0:T(8,128)S(1)}, u32[]{:S(2)}, u32[]{:S(2)}) collective-permute-start(f32[20,8,128]{2,1,0:T(8,128)S(1)} %get-tuple-element.19.refs_6_), channel_id=1, source_target_pairs={{0,1},{1,2},{2,3},{3,4},{4,5},{5,6},{6,7},{7,8},{8,9},{9,10},{10,1... | collective-permute-start | bytes 245768 | tf_op jit(solution)/shard_map/ppermute | solution.py:419
  126.8 2.4 %collective-permute-start.5 = (f32[20,8,128]{2,1,0:T(8,128)S(1)}, f32[20,8,128]{2,1,0:T(8,128)S(1)}, u32[]{:S(2)}, u32[]{:S(2)}) collective-permute-start(f32[20,8,128]{2,1,0:T(8,128)S(1)} %get-tuple-element.20.refs_5_), channel_id=1, source_target_pairs={{1,0},{2,1},{3,2},{4,3},{5,4},{6,5},{7,6},{8,7},{9,8},{10,9},{11,1... | collective-permute-start | bytes 245768 | tf_op jit(solution)/shard_map/ppermute | solution.py:419
  129.2 0.0 collective-permute-done.4.refs_4_
  129.3 7.6 %collective-permute-done.5.refs_7_ = f32[20,8,128]{2,1,0:T(8,128)S(1)} collective-permute-done((f32[20,8,128]{2,1,0:T(8,128)S(1)}, f32[20,8,128]{2,1,0:T(8,128)S(1)}, u32[]{:S(2)}, u32[]{:S(2)}) %collective-permute-start.5) | collective-permute-done | bytes 81952 | tf_op jit(solution)/shard_map/ppermute | solution.py:419
  136.8 20.0 %shard_map.117 = f32[3,5120]{1,0:T(4,128)} custom-call(s32[1]{0:T(128)} %bitcast.base_ref, s32[27,80]{1,0:T(8,128)S(1)} %copy-done, bf16[80,64,1792]{2,1,0:T(8,128)(2,1)} %get-tuple-element.15.hi, bf16[80,64,1792]{2,1,0:T(8,128)(2,1)} %get-tuple-element.16.lo, f32[20,128]{1,0:T(8,128)S(1)} %collective-permute-done.2.refs_0_, ...), custom_call_target="tpu_custom_call" | custom-call | tf_op jit(solution)/shard_map/pallas_call | solution.py:330
Async XLA Ops:
  0.6 0.9 copy-start.1
  1.5 0.9 copy-start.2
  2.4 0.9 copy-start.3
  3.3 0.7 copy-start.4
  4.0 0.7 copy-start.5
  4.8 0.7 copy-start.6
  5.5 0.7 copy-start.7
  6.1 0.7 copy-start.8
  6.8 0.7 copy-start.9
  33.1 8.6 %collective-permute-start = (f32[20,8,128]{2,1,0:T(8,128)S(1)}, f32[20,8,128]{2,1,0:T(8,128)S(1)}, u32[]{:S(2)}, u32[]{:S(2)}) collective-permute-start(f32[20,8,128]{2,1,0:T(8,128)S(1)} %get-tuple-element.13.tail.refs_6_.refs_9_), channel_id=1, source_target_pairs={{0,1},{1,2},{2,3},{3,4},{4,5},{5,6},{6,7},{7,8},{8,9},{9,10},{10,1... | collective-permute-start | bytes 245768 | tf_op jit(solution)/shard_map/ppermute | solution.py:419
  39.8 10.0 %collective-permute-start.1 = (f32[20,8,128]{2,1,0:T(8,128)S(1)}, f32[20,8,128]{2,1,0:T(8,128)S(1)}, u32[]{:S(2)}, u32[]{:S(2)}) collective-permute-start(f32[20,8,128]{2,1,0:T(8,128)S(1)} %get-tuple-element.14.head.refs_5_.refs_8_), channel_id=1, source_target_pairs={{1,0},{2,1},{3,2},{4,3},{5,4},{6,5},{7,6},{8,7},{9,8},{10,9},{11,1... | collective-permute-start | bytes 245768 | tf_op jit(solution)/shard_map/ppermute | solution.py:419
  49.8 0.7 copy-start
  94.0 4.3 %collective-permute-start.2 = (f32[20,128]{1,0:T(8,128)S(1)}, f32[20,128]{1,0:T(8,128)S(1)}, u32[]{:S(2)}, u32[]{:S(2)}) collective-permute-start(f32[20,128]{1,0:T(8,128)S(1)} %get-tuple-element.17.refs_2_), channel_id=1, source_target_pairs={{0,1},{1,2},{2,3},{3,4},{4,5},{5,6},{6,7},{7,8},{8,9},{9,10},{10,1... | collective-permute-start | bytes 30728 | tf_op jit(solution)/shard_map/ppermute | solution.py:419
  96.3 9.2 %collective-permute-start.3 = (f32[20,128]{1,0:T(8,128)S(1)}, f32[20,128]{1,0:T(8,128)S(1)}, u32[]{:S(2)}, u32[]{:S(2)}) collective-permute-start(f32[20,128]{1,0:T(8,128)S(1)} %get-tuple-element.18.refs_1_), channel_id=1, source_target_pairs={{1,0},{2,1},{3,2},{4,3},{5,4},{6,5},{7,6},{8,7},{9,8},{10,9},{11,1... | collective-permute-start | bytes 30728 | tf_op jit(solution)/shard_map/ppermute | solution.py:419
  124.9 4.3 %collective-permute-start.4 = (f32[20,8,128]{2,1,0:T(8,128)S(1)}, f32[20,8,128]{2,1,0:T(8,128)S(1)}, u32[]{:S(2)}, u32[]{:S(2)}) collective-permute-start(f32[20,8,128]{2,1,0:T(8,128)S(1)} %get-tuple-element.19.refs_6_), channel_id=1, source_target_pairs={{0,1},{1,2},{2,3},{3,4},{4,5},{5,6},{6,7},{7,8},{8,9},{9,10},{10,1... | collective-permute-start | bytes 245768 | tf_op jit(solution)/shard_map/ppermute | solution.py:419
  126.8 10.0 %collective-permute-start.5 = (f32[20,8,128]{2,1,0:T(8,128)S(1)}, f32[20,8,128]{2,1,0:T(8,128)S(1)}, u32[]{:S(2)}, u32[]{:S(2)}) collective-permute-start(f32[20,8,128]{2,1,0:T(8,128)S(1)} %get-tuple-element.20.refs_5_), channel_id=1, source_target_pairs={{1,0},{2,1},{3,2},{4,3},{5,4},{6,5},{7,6},{8,7},{9,8},{10,9},{11,1... | collective-permute-start | bytes 245768 | tf_op jit(solution)/shard_map/ppermute | solution.py:419

commit v2 on v1

--- a/solution.py
+++ b/solution.py
@@ -105,7 +105,10 @@
     copy.wait()
 
 
-def unpack_kernel(got, head, tail, count, heads_v, heads_s, store, sem):
+def unpack_kernel(got_hbm, head, tail, items, starts, count, heads_v, heads_s, store, got, sem):
+    copy = pltpu.make_async_copy(got_hbm, got, sem)
+    copy.start()
+    copy.wait()
     peers = got.shape[0] // PEER_ROWS
     pairs = store.shape[0] - 1
     heads = jnp.transpose(got[pl.ds(FIELDS, peers, stride=PEER_ROWS), :])
@@ -129,6 +132,17 @@
         return carry
 
     lax.fori_loop(0, peers, take, 0, unroll=8)
+    for index in range(items.shape[0]):
+        items[index] = 0
+
+    def list_items(cell, total):
+        starts[cell] = total
+        items[total] = 2 * cell
+        items[total + 1] = 2 * cell + 1
+        return total + 1 + (count[cell] > CHUNK).astype(jnp.int32)
+
+    total = lax.fori_loop(0, 2 * pairs, list_items, 0, unroll=8)
+    starts[2 * pairs] = (total + GROUP - 1) // GROUP
     head[...] = store[0 : pairs // 2]
     tail[...] = store[pairs // 2 : pairs]
 
@@ -147,25 +161,31 @@
     second[index + 1] = jnp.where(low, zero, tile).astype(first.dtype)
 
 
-def entries(adj, base, cell, dummy):
-    return [adj[n, cell] - base for n in ENTRY_ORDER] + [dummy]
+def over_items(groups, one_item):
+    def turn(step, carry):
+        for local in range(GROUP):
+            one_item(step, local)
+        return carry
+
+    lax.fori_loop(0, groups, turn, 0)
+
+
+def entries(adj, cell, dummy):
+    return [adj[n, cell] for n in range(NEIGH)] + [dummy]
 
 
 def density_kernel(
-    base_ref, adj, count, left, head, tail, right, hi, lo, dens, coef_head, coef_tail,
+    items, starts, adj, left, head, tail, right, hi, lo, dens, coef_head, coef_tail,
     terms_a, terms_b, ext, stage, lhs, own_r, rows_t, rows_f, acc, raw,
 ):
     rim = 2 * head.shape[0]
     quarter = head.shape[0]
     dummy = 4 * rim
-    base = base_ref[0]
-    step = pl.program_id(0)
     low8 = lane_iota((FIELDS, 128)) < SLOTS
     low32 = lane_iota((TERMS, 128)) < SLOTS
     sub8 = sub_iota((FIELDS, 128))
 
-    @pl.when(step == 0)
-    def _():
+    if True:
         ext[dummy] = jnp.where(sub8 == 7, 1.0, 0.0)
         terms_a[dummy] = jnp.zeros((TERMS, 128), BF16)
         terms_b[dummy] = jnp.zeros((TERMS, 128), BF16)
@@ -197,55 +217,52 @@
                     extra = jnp.where(sub8 == 0, a1, jnp.where(sub8 == 1, a2, a3))
                     stage[at, 24:32, :] = jnp.where(sub8 < 3, extra, tile[7:8])
                     turned = jnp.transpose(stage[at])
-                    lhs[own] = turned.astype(BF16)
-                    own_r[own] = jnp.broadcast_to(turned[:, 31:32], (128, 128))
+                    radius = jnp.broadcast_to(turned[:, 31:32], (128, 128))
+                    lhs[4 * own : 4 * own + 4] = turned.astype(BF16).reshape(4, CHUNK, TERMS)
+                    own_r[4 * own : 4 * own + 4] = radius.reshape(4, CHUNK, 128)
 
     chunk_lane = lane_iota((CHUNK, 128))
     chunk_sub = sub_iota((CHUNK, 128))
 
-    def one_cell(local, carry):
-        cell = step * GROUP + local
-        index = entries(adj, base, cell, dummy)
+    def one_item(step, local):
+        place = step * GROUP + local
+        item = items[place]
+        cell = item // 2
+        at = local
+        index = entries(adj, cell, dummy)
         for p in range(ROWS):
             i, j = index[2 * p], index[2 * p + 1]
-            rows_f[p] = jnp.where(low8, ext[i], ext[j])
-            rows_t[:, p * 128 : p * 128 + 128] = terms_a[i] + terms_b[j]
-
-        def turn(part, carry):
-            first = pl.multiple_of(part * CHUNK, CHUNK)
-            place = pl.multiple_of(lax.rem(cell, 2) * SLOTS + first, CHUNK)
-            own = lhs[cell // 2, pl.ds(place, CHUNK), :]
-            ri = own_r[cell // 2, pl.ds(place, CHUNK), :]
-            total = jnp.zeros((CHUNK, 128), F32)
-            for p2 in range(ROWS // 2):
-                wide = jnp.dot(
-                    own, rows_t[:, p2 * 256 : p2 * 256 + 256], preferred_element_type=F32
-                )
-                for p in (2 * p2, 2 * p2 + 1):
-                    q = jnp.maximum(wide[:, (p % 2) * 128 : (p % 2) * 128 + 128], 0.0)
-                    q2 = q * q
-                    total = total + q2 * (q * rows_f[p, 6:7, :])
-                    value = q2 * pl.reciprocal(ri + rows_f[p, 7:8, :])
-                    if p == 0:
-                        value = jnp.where(chunk_lane == chunk_sub + first, 0.0, value)
-                    upper = value.astype(BF16)
-                    span = slice(p * 128, p * 128 + 128)
-                    hi[local, pl.ds(first, CHUNK), span] = upper
-                    lo[local, pl.ds(first, CHUNK), span] = (value - upper.astype(F32)).astype(BF16)
-            acc[cell, pl.ds(first, CHUNK), :] = total
-            return carry
-
-        return lax.fori_loop(0, (count[cell] + CHUNK - 1) // CHUNK, turn, carry)
-
-    lax.fori_loop(0, GROUP, one_cell, 0)
-
-    @pl.when(step == pl.num_programs(0) - 1)
-    def _():
+            rows_f[at, p] = jnp.where(low8, ext[i], ext[j])
+            rows_t[at, :, p * 128 : p * 128 + 128] = terms_a[i] + terms_b[j]
+        own = lhs[item]
+        ri = own_r[item]
+        first = (item - 2 * cell) * CHUNK
+        total = jnp.zeros((CHUNK, 128), F32)
+        for p2 in range(ROWS // 2):
+            wide = jnp.dot(
+                own, rows_t[at, :, p2 * 256 : p2 * 256 + 256], preferred_element_type=F32
+            )
+            for p in (2 * p2, 2 * p2 + 1):
+                q = jnp.maximum(wide[:, (p % 2) * 128 : (p % 2) * 128 + 128], 0.0)
+                q2 = q * q
+                total = total + q2 * (q * rows_f[at, p, 6:7, :])
+                value = q2 * pl.reciprocal(ri + rows_f[at, p, 7:8, :])
+                if p == 0:
+                    value = jnp.where(chunk_lane == chunk_sub + first, 0.0, value)
+                upper = value.astype(BF16)
+                span = slice(p * 128, p * 128 + 128)
+                hi[place, :, span] = upper
+                lo[place, :, span] = (value - upper.astype(F32)).astype(BF16)
+        acc[item] = total
+
+    over_items(starts[4 * quarter], one_item)
+
+    if True:
         ones = jnp.ones((FIELDS, 128), BF16)
 
         def reduce_pair(pair, carry):
             total = jnp.zeros((FIELDS, 128), F32)
-            for part in split_bf16(acc[pl.ds(2 * pair, 2)].reshape(2 * SLOTS, 128), 3):
+            for part in split_bf16(acc[pl.ds(4 * pair, 4)].reshape(2 * SLOTS, 128), 3):
                 total = total + lax.dot_general(
                     ones, part.astype(BF16), (((1,), (1,)), ((), ())), preferred_element_type=F32
                 )
@@ -261,7 +278,7 @@
             coef[...] = (2.0 * visc_scale) * mass / jnp.where(live, value, 1.0)
 
 
-def sweep_kernel(is_first, base_ref, adj, hi, lo, *refs):
+def sweep_kernel(is_first, items, starts, adj, hi, lo, *refs):
     coefs, speeds, refs = refs[:4], refs[4:8], refs[8:]
     if is_first:
         (head, tail), (out_head, out_tail), refs = speeds[1:3], refs[:2], refs[2:]
@@ -271,15 +288,13 @@
     quarter = head.shape[0]
     rim = 2 * quarter
     dummy = 4 * rim
-    base = base_ref[0]
-    step = pl.program_id(0)
     low = lane_iota((FIELDS, 128)) < SLOTS
     low16 = lane_iota((2 * FIELDS, 128)) < SLOTS
+    eighth = lane_iota((FIELDS, 128)) // CHUNK
     sub = sub_iota((FIELDS, 128))
     moving = (sub >= 3) & (sub < 6)
 
-    @pl.when(step == 0)
-    def _():
+    if True:
         ext_a[dummy] = jnp.zeros((2 * FIELDS, 128), BF16)
         ext_b[dummy] = jnp.zeros((2 * FIELDS, 128), BF16)
         for part in range(4):
@@ -291,29 +306,30 @@
                 stage[at, FIELDS:, :] = w2
                 put_halves(stage[at], low16, ext_a, ext_b, part * rim + 2 * pair)
 
-    def one_cell(local, carry):
-        cell = step * GROUP + local
-        index = entries(adj, base, cell, dummy)
-        at = lax.rem(local, 4)
+    def one_item(step, local):
+        place = step * GROUP + local
+        index = entries(adj, items[place] // 2, dummy)
+        at = local
         for p in range(ROWS):
             rows[at, :, p * 128 : p * 128 + 128] = ext_a[index[2 * p]] + ext_b[index[2 * p + 1]]
-        total = jnp.zeros((2 * FIELDS, SLOTS), F32)
+        total = jnp.zeros((2 * FIELDS, CHUNK), F32)
         for part in (hi, lo):
             total = total + lax.dot_general(
-                rows[at], part[local], (((1,), (1,)), ((), ())), preferred_element_type=F32
+                rows[at], part[place], (((1,), (1,)), ((), ())), preferred_element_type=F32
             )
-        sums[cell, :, 0:SLOTS] = total[0:FIELDS] + total[FIELDS:]
-        return carry
-
-    lax.fori_loop(0, GROUP, one_cell, 0, unroll=4)
-
-    @pl.when(step == pl.num_programs(0) - 1)
-    def _():
+        sums[place, :, 0:CHUNK] = total[0:FIELDS] + total[FIELDS:]
+
+    over_items(starts[2 * rim], one_item)
+
+    if True:
         for part, ref in enumerate((head, tail)):
             for pair in range(quarter):
                 slot = part * quarter + pair
                 tile = ref[pair]
-                total = jnp.where(low, sums[2 * slot], pltpu.roll(sums[2 * slot + 1], SLOTS, 1))
+                total = sums[starts[2 * slot]]
+                for n in range(1, 4):
+                    place = starts[2 * slot + n // 2] + n % 2
+                    total = jnp.where(eighth == n, pltpu.roll(sums[place], n * CHUNK, 1), total)
                 live = jnp.broadcast_to(tile[6:7] > 0.0, (FIELDS, 128))
                 rate = mass_rate * tile[6:7]
                 below = jnp.broadcast_to(rate + total[0:1], (FIELDS, 128))
@@ -325,16 +341,18 @@
                     out[:, slot * 128 : slot * 128 + 128] = value[3:6]
 
 
-def call(kernel, outs, scratch, in_specs, args, out_specs=None, grid=None, vmem=40):
-    extra = {} if grid is None else {"grid": grid}
+def call(kernel, outs, scratch, in_specs, args, out_specs, grid=(), scalars=0, vmem=40):
     return pl.pallas_call(
         kernel,
         out_shape=outs,
-        in_specs=in_specs,
-        out_specs=out_specs,
-        scratch_shapes=scratch,
+        grid_spec=pltpu.PrefetchScalarGridSpec(
+            num_scalar_prefetch=scalars,
+            grid=grid,
+            in_specs=in_specs,
+            out_specs=out_specs,
+            scratch_shapes=scratch,
+        ),
         compiler_params=pltpu.CompilerParams(vmem_limit_bytes=vmem * MIB),
-        **extra,
     )(*args)
 
 
@@ -347,43 +365,44 @@
 
 
 def whole(*shape):
-    return pl.BlockSpec(shape, lambda g: (0,) * len(shape))
-
-
-def density(base, adj, count, left, head, tail, right):
+    return pl.BlockSpec(shape, lambda *scalars: (0,) * len(shape))
+
+
+def density(items, starts, adj, left, head, tail, right):
     quarter = head.shape[0]
     cells, pairs = 4 * quarter, 2 * quarter
     ext = 2 * cells + 1
     tile = whole(quarter, FIELDS, 128)
-    block = pl.BlockSpec((GROUP, SLOTS, WIDTH), lambda g: (g, 0, 0))
+    block = spec(VMEM)
     return call(
         density_kernel,
-        [jax.ShapeDtypeStruct((cells, SLOTS, WIDTH), BF16)] * 2
+        [pltpu.VMEM((2 * cells, CHUNK, WIDTH), BF16)] * 2
         + [f32(pairs, 128), f32(quarter, 128), f32(quarter, 128)],
         [pltpu.VMEM((ext, TERMS, 128), BF16)] * 2
         + [
             pltpu.VMEM((ext, FIELDS, 128), F32),
             pltpu.VMEM((16, TERMS, 128), F32),
-            pltpu.VMEM((pairs, 128, TERMS), BF16),
-            pltpu.VMEM((pairs, 128, 128), F32),
-            pltpu.VMEM((TERMS, WIDTH), BF16),
-            pltpu.VMEM((ROWS, FIELDS, 128), F32),
-            pltpu.VMEM((cells, SLOTS, 128), F32),
+            pltpu.VMEM((2 * cells, CHUNK, TERMS), BF16),
+            pltpu.VMEM((2 * cells, CHUNK, 128), F32),
+            pltpu.VMEM((GROUP, TERMS, WIDTH), BF16),
+            pltpu.VMEM((GROUP, ROWS, FIELDS, 128), F32),
+            pltpu.VMEM((2 * cells, CHUNK, 128), F32),
             pltpu.VMEM((pairs, 128), F32),
         ],
-        [spec(SMEM)] * 3 + [tile] * 4,
-        (base, adj, count, left, head, tail, right),
+        [tile] * 4,
+        (items, starts, adj, left, head, tail, right),
         out_specs=[block] * 2 + [whole(pairs, 128), whole(quarter, 128), whole(quarter, 128)],
-        grid=(cells // GROUP,),
-    )
-
-
-def sweep(is_first, base, adj, hi, lo, coefs, speeds, head, tail):
+        vmem=22,
+        scalars=3,
+    )
+
+
+def sweep(is_first, items, starts, adj, hi, lo, coefs, speeds, head, tail):
     quarter = head.shape[0]
     cells = 4 * quarter
     ext = 2 * cells + 1
     tile = whole(quarter, FIELDS, 128)
-    block = pl.BlockSpec((GROUP, SLOTS, WIDTH), lambda g: (g, 0, 0))
+    block = spec(VMEM)
     own = () if is_first else (head, tail)
     if is_first:
         outs, out_specs = [f32(quarter, FIELDS, 128)] * 2, [tile] * 2
@@ -394,14 +413,15 @@
         outs,
         [pltpu.VMEM((ext, 2 * FIELDS, 128), BF16)] * 2
         + [
-            pltpu.VMEM((4, 2 * FIELDS, WIDTH), BF16),
-            pltpu.VMEM((cells, FIELDS, 128), F32),
+            pltpu.VMEM((GROUP, 2 * FIELDS, WIDTH), BF16),
+            pltpu.VMEM((2 * cells + GROUP, FIELDS, 128), F32),
             pltpu.VMEM((8, 2 * FIELDS, 128), F32),
         ],
-        [spec(SMEM)] * 2 + [block] * 2 + [whole(quarter, 128)] * 4 + [tile] * (4 + len(own)),
-        (base, adj, hi, lo) + tuple(coefs) + tuple(speeds) + own,
+        [block] * 2 + [whole(quarter, 128)] * 4 + [tile] * (4 + len(own)),
+        (items, starts, adj, hi, lo) + tuple(coefs) + tuple(speeds) + own,
         out_specs=out_specs,
-        grid=(cells // GROUP,),
+        vmem=22,
+        scalars=3,
     )
 
 
@@ -420,6 +440,7 @@
 
     args = (tally, peer, place, pos, speed, force)
     args = args + tuple(v.reshape(pairs, 128) for v in (weight, heat, share))
+    args = tuple(pltpu.with_memory_space_constraint(v, HBM) for v in args)
     (sent,) = call(
         pack_kernel,
         [pltpu.HBM((peers * PEER_ROWS, 128), F32)],
@@ -431,37 +452,42 @@
             pltpu.SemaphoreType.DMA((9,)),
             pltpu.SemaphoreType.DMA,
         ],
-        [spec(pl.ANY)] * 9,
+        [spec(HBM)] * 9,
         args,
         out_specs=[spec(HBM)],
     )
     got = lax.all_to_all(
         sent.reshape(peers, 1, PEER_ROWS * 128), "cells", split_axis=0, concat_axis=0, tiled=True
     )
-    head, tail, count = call(
+    head, tail, items, starts = call(
         unpack_kernel,
-        [f32(quarter, FIELDS, 128)] * 2 + [jax.ShapeDtypeStruct((cells + 1,), jnp.int32)],
+        [f32(quarter, FIELDS, 128)] * 2
+        + [jax.ShapeDtypeStruct((n,), jnp.int32) for n in (2 * cells + GROUP, cells + 1)],
         [
+            pltpu.SMEM((cells + 1,), jnp.int32),
             pltpu.VMEM((4, 128), jnp.int32),
             pltpu.SMEM((4, 128), jnp.int32),
             pltpu.VMEM((pairs + 1, FIELDS, 128), F32),
+            pltpu.VMEM((peers * PEER_ROWS, 128), F32),
             pltpu.SemaphoreType.DMA,
         ],
-        [spec(VMEM)],
+        [spec(HBM)],
         (got.reshape(peers * PEER_ROWS, 128),),
-        out_specs=[spec(VMEM)] * 2 + [spec(SMEM)],
+        out_specs=[spec(VMEM)] * 2 + [spec(SMEM)] * 2,
     )
     left, right = rims(head, tail)
-    base = (rank * cells - rim).astype(jnp.int32).reshape(1)
-    hi, lo, dens, coef_head, coef_tail = density(base, adj, count, left, head, tail, right)
+    local = adj - (rank * cells - rim).astype(jnp.int32)
+    adj = jnp.concatenate([local[13:14], local[:13], local[14:]], axis=0)
+    hi, lo, dens, coef_head, coef_tail = density(items, starts, adj, left, head, tail, right)
+    hi, lo = (pltpu.with_memory_space_constraint(v, VMEM) for v in (hi, lo))
     coef_left, coef_right = rims(coef_head, coef_tail)
     coefs = (coef_left, coef_head, coef_tail, coef_right)
     first_head, first_tail = sweep(
-        True, base, adj, hi, lo, coefs, (left, head, tail, right), head, tail
+        True, items, starts, adj, hi, lo, coefs, (left, head, tail, right), head, tail
     )
     first_left, first_right = rims(first_head, first_tail)
     speeds = (first_left, first_head, first_tail, first_right)
-    (out,) = sweep(False, base, adj, hi, lo, coefs, speeds, head, tail)
+    (out,) = sweep(False, items, starts, adj, hi, lo, coefs, speeds, head, tail)
     return out, dens.reshape(cells * SLOTS)
 
 

time: 157 us -> 129 us (0.82)
  Pallas kernels: 88.8 us -> 63.4 us
  blocking collectives: 19.7 us -> 0 us
  starting transfers between devices: 17.2 us -> 28.2 us
  waiting for transfers between devices: 22.8 us -> 32.1 us
  local copies, waits for them, and re-layouts: 7.51 us -> 1.84 us
    pallas_call x5, Pallas kernels: 88.8 us -> 63.4 us  [call(): pl.pallas_call(kernel, out_shape=outs, grid_spec=pltpu.PrefetchScalarGrid...]
    all_to_all x1 -> x0, blocking collectives: 19.7 us -> none  [body(): lax.all_to_all(sent.reshape(peers, 1, PEER_ROWS * 128), 'cells', split_ax...]
    all_to_all x0 -> x1, starting transfers between devices: none -> 10 us  [body(): lax.all_to_all(sent.reshape(peers, 1, PEER_ROWS * 128), 'cells', split_ax...]
    all_to_all x0 -> x1, waiting for transfers between devices: none -> 8.96 us  [body(): lax.all_to_all(sent.reshape(peers, 1, PEER_ROWS * 128), 'cells', split_ax...]
    unnamed x20, local copies, waits for them, and re-layouts: 7.51 us -> 1.83 us
  transfers between devices with their start and end apart: 6 -> 7, of which waited for: 3 -> 4; matrix products, arithmetic and copies ran while one was open for 0% -> 1% of each run, Pallas kernels for 0% -> 0%
where the time goes in v2:
time: 129 us; the launch traced here: 128 us
  Pallas kernels  63.4 us (49%)
  waiting for transfers between devices  32.1 us (25%)
  starting transfers between devices  28.2 us (22%)
  local copies, waits for them, and re-layouts  1.84 us (1%)
  other arithmetic  1.33 us (1%)
    pallas_call x5, Pallas kernels, call(): pl.pallas_call(kernel, out_shape=outs, grid_spec=pltpu.PrefetchScalarGrid...  63.4 us
    ppermute x3, waiting for transfers between devices, rims(): lax.ppermute(head, 'cells', left_going)  23.2 us
    ppermute x3, starting transfers between devices, rims(): lax.ppermute(tail, 'cells', right_going)  12.4 us
    all_to_all x1, starting transfers between devices, body(): lax.all_to_all(sent.reshape(peers, 1, PEER_ROWS * 128), 'cells', split_ax...  10 us
    all_to_all x1, waiting for transfers between devices, body(): lax.all_to_all(sent.reshape(peers, 1, PEER_ROWS * 128), 'cells', split_ax...  8.96 us
    ppermute x3, starting transfers between devices, rims(): lax.ppermute(head, 'cells', left_going)  5.76 us
  transfers between devices with their start and end apart: 7, of which 4 were waited for; matrix products, arithmetic and copies ran while one was open for 1% of the time, Pallas kernels for 0%

profile of v2, /device:TPU:121, one launch (start us, length us, event | category | flops | bytes accessed | tf_op | source)
XLA Modules:
  0.0 127.7 jit_solution(9790042607301224399)
XLA Ops:
  0.6 2.7 %shard_map.113 = f32[1152,128]{1,0:T(8,128)} custom-call(s32[80]{0:T(128)} %refs_0_.1, s32[80]{0:T(128)} %refs_1_.1, s32[80]{0:T(128)} %refs_2_.1, f32[3,5120]{1,0:T(4,128)} %refs_3_.1, f32[3,5120]{1,0:T(4,128)} %refs_4_.1, f32[3,5120]{1,0:T(4,128)} %refs_5_.1, f32[40,128]{1,0:T(8,128)} %bitcast.8, f32[40,128]{1,0:T(8,128)} %bitcast.9, f32[40,128]{1,0:T(8,128)} %bitcast.10), custom_call_target="tpu_custom_call" | custom-call | tf_op jit(solution)/shard_map/pallas_call | solution.py:345
  3.4 10.0 %all-to-all-start = ((f32[128,1,1152]{2,1,0:T(1,128)}), f32[128,1,1152]{2,1,0:T(1,128)S(1)}, u32[]{:S(2)}, u32[]{:S(2)}) async-start(f32[128,1,1152]{2,1,0:T(1,128)} %bitcast.7), calls=%async_computation | async-start | bytes 1179648 | tf_op jit(solution)/shard_map/all_to_all | solution.py:459
  13.4 0.7 broadcast_subtract_fusion
  14.1 9.0 %all-to-all-done = f32[128,1,1152]{2,1,0:T(1,128)S(1)} async-done(((f32[128,1,1152]{2,1,0:T(1,128)}), f32[128,1,1152]{2,1,0:T(1,128)S(1)}, u32[]{:S(2)}, u32[]{:S(2)}) %all-to-all-start) | async-done | bytes 589856 | tf_op jit(solution)/shard_map/all_to_all | solution.py:459
  23.1 4.2 %shard_map.114 = (f32[20,8,128]{2,1,0:T(8,128)S(1)}, f32[20,8,128]{2,1,0:T(8,128)S(1)}, s32[168]{0:T(256)S(1)}, s32[81]{0:T(128)S(1)}) custom-call(f32[1152,128]{1,0:T(8,128)S(1)} %bitcast.6), custom_call_target="tpu_custom_call" | custom-call | tf_op jit(solution)/shard_map/pallas_call | solution.py:345
  27.4 0.0 copy-start.2
  27.4 0.0 copy-start
  27.4 0.0 copy-start.1
  27.4 0.0 copy-start.3
  27.4 6.7 %collective-permute-start = (f32[20,8,128]{2,1,0:T(8,128)S(1)}, f32[20,8,128]{2,1,0:T(8,128)S(1)}, u32[]{:S(2)}, u32[]{:S(2)}) collective-permute-start(f32[20,8,128]{2,1,0:T(8,128)S(1)} %get-tuple-element.15.tail.refs_6_.refs_9_), channel_id=1, source_target_pairs={{0,1},{1,2},{2,3},{3,4},{4,5},{5,6},{6,7},{7,8},{8,9},{9,10},{10,1... | collective-permute-start | bytes 245768 | tf_op jit(solution)/shard_map/ppermute | solution.py:439
  34.1 1.9 %collective-permute-start.1 = (f32[20,8,128]{2,1,0:T(8,128)S(1)}, f32[20,8,128]{2,1,0:T(8,128)S(1)}, u32[]{:S(2)}, u32[]{:S(2)}) collective-permute-start(f32[20,8,128]{2,1,0:T(8,128)S(1)} %get-tuple-element.16.head.refs_5_.refs_8_), channel_id=1, source_target_pairs={{1,0},{2,1},{3,2},{4,3},{5,4},{6,5},{7,6},{8,7},{9,8},{10,9},{11,1... | collective-permute-start | bytes 245768 | tf_op jit(solution)/shard_map/ppermute | solution.py:439
  36.0 0.6 pad_add_fusion.adj
  36.6 0.0 collective-permute-done.left.refs_4_
  36.6 0.0 copy-start.4
  36.6 7.4 %collective-permute-done.1.right.refs_7_ = f32[20,8,128]{2,1,0:T(8,128)S(1)} collective-permute-done((f32[20,8,128]{2,1,0:T(8,128)S(1)}, f32[20,8,128]{2,1,0:T(8,128)S(1)}, u32[]{:S(2)}, u32[]{:S(2)}) %collective-permute-start.1) | collective-permute-done | bytes 81952 | tf_op jit(solution)/shard_map/ppermute | solution.py:439
  44.0 0.0 copy-start.5
  44.0 0.0 copy-done.2
  44.1 0.0 copy-done
  44.1 0.0 copy-done.1
  44.1 0.0 copy-done.3
  44.1 0.0 copy-done.4
  44.1 0.6 copy-done.5
  44.7 29.2 %shard_map.115 = (bf16[160,32,1792]{2,1,0:T(8,128)(2,1)S(1)}, bf16[160,32,1792]{2,1,0:T(8,128)(2,1)S(1)}, f32[40,128]{1,0:T(8,128)}, f32[20,128]{1,0:T(8,128)}, f32[20,128]{1,0:T(8,128)}) custom-call(s32[168]{0:T(256)} %copy-done.2, s32[81]{0:T(128)} %copy-done.3, s32[27,80]{1,0:T(8,128)} %pad_add_fusion.adj, f32[20,8,128]{2,1,0:T(8,128)} %copy-done.4, ...), custom_call_target="tpu_custom_call" | custom-call | tf_op jit(solution)/shard_map/pallas_call | solution.py:345
  73.9 3.2 %collective-permute-start.2 = (f32[20,128]{1,0:T(8,128)}, f32[20,128]{1,0:T(8,128)S(1)}, u32[]{:S(2)}, u32[]{:S(2)}) collective-permute-start(f32[20,128]{1,0:T(8,128)} %get-tuple-element.19.refs_2_), channel_id=1, source_target_pairs={{0,1},{1,2},{2,3},{3,4},{4,5},{5,6},{6,7},{7,8},{8,9},{9,10},{10,1... | collective-permute-start | bytes 30728 | tf_op jit(solution)/shard_map/ppermute | solution.py:439
  77.1 1.9 %collective-permute-start.3 = (f32[20,128]{1,0:T(8,128)}, f32[20,128]{1,0:T(8,128)S(1)}, u32[]{:S(2)}, u32[]{:S(2)}) collective-permute-start(f32[20,128]{1,0:T(8,128)} %get-tuple-element.20.refs_1_), channel_id=1, source_target_pairs={{1,0},{2,1},{3,2},{4,3},{5,4},{6,5},{7,6},{8,7},{9,8},{10,9},{11,1... | collective-permute-start | bytes 30728 | tf_op jit(solution)/shard_map/ppermute | solution.py:439
  79.0 0.0 collective-permute-done.2.refs_0_
  79.0 0.0 copy-start.8
  79.0 7.5 %collective-permute-done.3.refs_3_ = f32[20,128]{1,0:T(8,128)S(1)} collective-permute-done((f32[20,128]{1,0:T(8,128)}, f32[20,128]{1,0:T(8,128)S(1)}, u32[]{:S(2)}, u32[]{:S(2)}) %collective-permute-start.3) | collective-permute-done | bytes 10272 | tf_op jit(solution)/shard_map/ppermute | solution.py:439
  86.5 0.0 copy-start.9
  86.5 0.0 copy-done.8
  86.5 0.6 copy-done.9
  87.1 13.5 %shard_map.116 = (f32[20,8,128]{2,1,0:T(8,128)}, f32[20,8,128]{2,1,0:T(8,128)}) custom-call(s32[168]{0:T(256)} %copy-done.2, s32[81]{0:T(128)} %copy-done.3, s32[27,80]{1,0:T(8,128)} %pad_add_fusion.adj, bf16[160,32,1792]{2,1,0:T(8,128)(2,1)S(1)} %get-tuple-element.17.hi, bf16[160,32,1792]{2,1,0:T(8,128)(2,1)S(1)} %get-tuple-element.18.lo, ...), custom_call_target="tpu_custom_call" | custom-call | tf_op jit(solution)/shard_map/pallas_call | solution.py:345
  100.7 2.6 %collective-permute-start.4 = (f32[20,8,128]{2,1,0:T(8,128)}, f32[20,8,128]{2,1,0:T(8,128)S(1)}, u32[]{:S(2)}, u32[]{:S(2)}) collective-permute-start(f32[20,8,128]{2,1,0:T(8,128)} %get-tuple-element.21.refs_6_), channel_id=1, source_target_pairs={{0,1},{1,2},{2,3},{3,4},{4,5},{5,6},{6,7},{7,8},{8,9},{9,10},{10,1... | collective-permute-start | bytes 245768 | tf_op jit(solution)/shard_map/ppermute | solution.py:439
  103.2 1.9 %collective-permute-start.5 = (f32[20,8,128]{2,1,0:T(8,128)}, f32[20,8,128]{2,1,0:T(8,128)S(1)}, u32[]{:S(2)}, u32[]{:S(2)}) collective-permute-start(f32[20,8,128]{2,1,0:T(8,128)} %get-tuple-element.22.refs_5_), channel_id=1, source_target_pairs={{1,0},{2,1},{3,2},{4,3},{5,4},{6,5},{7,6},{8,7},{9,8},{10,9},{11,1... | collective-permute-start | bytes 245768 | tf_op jit(solution)/shard_map/ppermute | solution.py:439
  105.2 0.0 collective-permute-done.4.refs_4_
  105.2 0.0 copy-start.6
  105.2 8.2 %collective-permute-done.5.refs_7_ = f32[20,8,128]{2,1,0:T(8,128)S(1)} collective-permute-done((f32[20,8,128]{2,1,0:T(8,128)}, f32[20,8,128]{2,1,0:T(8,128)S(1)}, u32[]{:S(2)}, u32[]{:S(2)}) %collective-permute-start.5) | collective-permute-done | bytes 81952 | tf_op jit(solution)/shard_map/ppermute | solution.py:439
  113.4 0.0 copy-done.6
  113.4 0.0 copy-start.7
  113.4 0.6 copy-done.7
  114.1 13.6 %shard_map.117 = f32[3,5120]{1,0:T(4,128)} custom-call(s32[168]{0:T(256)} %copy-done.2, s32[81]{0:T(128)} %copy-done.3, s32[27,80]{1,0:T(8,128)} %pad_add_fusion.adj, bf16[160,32,1792]{2,1,0:T(8,128)(2,1)S(1)} %get-tuple-element.17.hi, bf16[160,32,1792]{2,1,0:T(8,128)(2,1)S(1)} %get-tuple-element.18.lo, f32[20,128]{1,0:T(8,128)} %copy-done.8, ...), custom_call_target="tpu_custom_call" | custom-call | tf_op jit(solution)/shard_map/pallas_call | solution.py:345
  (2 shorter events, 0.0 us)
Async XLA Ops:
  3.4 19.7 %all-to-all-start = ((f32[128,1,1152]{2,1,0:T(1,128)}), f32[128,1,1152]{2,1,0:T(1,128)S(1)}, u32[]{:S(2)}, u32[]{:S(2)}) async-start(f32[128,1,1152]{2,1,0:T(1,128)} %bitcast.7), calls=%async_computation | async-start | bytes 1179648 | tf_op jit(solution)/shard_map/all_to_all | solution.py:459
  27.4 16.7 %copy-start.2 = (s32[168]{0:T(256)}, s32[168]{0:T(256)S(1)}, u32[]{:S(2)}) copy-start(s32[168]{0:T(256)S(1)} %get-tuple-element.13.items) | copy-start | bytes 2020
  27.4 16.7 %copy-start = (f32[20,8,128]{2,1,0:T(8,128)}, f32[20,8,128]{2,1,0:T(8,128)S(1)}, u32[]{:S(2)}) copy-start(f32[20,8,128]{2,1,0:T(8,128)S(1)} %get-tuple-element.16.head.refs_5_.refs_8_) | copy-start | bytes 245764
  27.4 16.7 %copy-start.1 = (f32[20,8,128]{2,1,0:T(8,128)}, f32[20,8,128]{2,1,0:T(8,128)S(1)}, u32[]{:S(2)}) copy-start(f32[20,8,128]{2,1,0:T(8,128)S(1)} %get-tuple-element.15.tail.refs_6_.refs_9_) | copy-start | bytes 245764
  27.4 16.7 %copy-start.3 = (s32[81]{0:T(128)}, s32[81]{0:T(128)S(1)}, u32[]{:S(2)}) copy-start(s32[81]{0:T(128)S(1)} %get-tuple-element.14.starts) | copy-start | bytes 976
  27.4 9.2 %collective-permute-start = (f32[20,8,128]{2,1,0:T(8,128)S(1)}, f32[20,8,128]{2,1,0:T(8,128)S(1)}, u32[]{:S(2)}, u32[]{:S(2)}) collective-permute-start(f32[20,8,128]{2,1,0:T(8,128)S(1)} %get-tuple-element.15.tail.refs_6_.refs_9_), channel_id=1, source_target_pairs={{0,1},{1,2},{2,3},{3,4},{4,5},{5,6},{6,7},{7,8},{8,9},{9,10},{10,1... | collective-permute-start | bytes 245768 | tf_op jit(solution)/shard_map/ppermute | solution.py:439
  34.1 10.0 %collective-permute-start.1 = (f32[20,8,128]{2,1,0:T(8,128)S(1)}, f32[20,8,128]{2,1,0:T(8,128)S(1)}, u32[]{:S(2)}, u32[]{:S(2)}) collective-permute-start(f32[20,8,128]{2,1,0:T(8,128)S(1)} %get-tuple-element.16.head.refs_5_.refs_8_), channel_id=1, source_target_pairs={{1,0},{2,1},{3,2},{4,3},{5,4},{6,5},{7,6},{8,7},{9,8},{10,9},{11,1... | collective-permute-start | bytes 245768 | tf_op jit(solution)/shard_map/ppermute | solution.py:439
  36.6 7.5 %copy-start.4 = (f32[20,8,128]{2,1,0:T(8,128)}, f32[20,8,128]{2,1,0:T(8,128)S(1)}, u32[]{:S(2)}) copy-start(f32[20,8,128]{2,1,0:T(8,128)S(1)} %collective-permute-done.left.refs_4_) | copy-start | bytes 245764
  44.0 0.6 copy-start.5
  73.9 5.1 %collective-permute-start.2 = (f32[20,128]{1,0:T(8,128)}, f32[20,128]{1,0:T(8,128)S(1)}, u32[]{:S(2)}, u32[]{:S(2)}) collective-permute-start(f32[20,128]{1,0:T(8,128)} %get-tuple-element.19.refs_2_), channel_id=1, source_target_pairs={{0,1},{1,2},{2,3},{3,4},{4,5},{5,6},{6,7},{7,8},{8,9},{9,10},{10,1... | collective-permute-start | bytes 30728 | tf_op jit(solution)/shard_map/ppermute | solution.py:439
  77.1 9.4 %collective-permute-start.3 = (f32[20,128]{1,0:T(8,128)}, f32[20,128]{1,0:T(8,128)S(1)}, u32[]{:S(2)}, u32[]{:S(2)}) collective-permute-start(f32[20,128]{1,0:T(8,128)} %get-tuple-element.20.refs_1_), channel_id=1, source_target_pairs={{1,0},{2,1},{3,2},{4,3},{5,4},{6,5},{7,6},{8,7},{9,8},{10,9},{11,1... | collective-permute-start | bytes 30728 | tf_op jit(solution)/shard_map/ppermute | solution.py:439
  79.0 7.5 %copy-start.8 = (f32[20,128]{1,0:T(8,128)}, f32[20,128]{1,0:T(8,128)S(1)}, u32[]{:S(2)}) copy-start(f32[20,128]{1,0:T(8,128)S(1)} %collective-permute-done.2.refs_0_) | copy-start | bytes 30724
  86.5 0.6 copy-start.9
  100.7 4.5 %collective-permute-start.4 = (f32[20,8,128]{2,1,0:T(8,128)}, f32[20,8,128]{2,1,0:T(8,128)S(1)}, u32[]{:S(2)}, u32[]{:S(2)}) collective-permute-start(f32[20,8,128]{2,1,0:T(8,128)} %get-tuple-element.21.refs_6_), channel_id=1, source_target_pairs={{0,1},{1,2},{2,3},{3,4},{4,5},{5,6},{6,7},{7,8},{8,9},{9,10},{10,1... | collective-permute-start | bytes 245768 | tf_op jit(solution)/shard_map/ppermute | solution.py:439
  103.2 10.2 %collective-permute-start.5 = (f32[20,8,128]{2,1,0:T(8,128)}, f32[20,8,128]{2,1,0:T(8,128)S(1)}, u32[]{:S(2)}, u32[]{:S(2)}) collective-permute-start(f32[20,8,128]{2,1,0:T(8,128)} %get-tuple-element.22.refs_5_), channel_id=1, source_target_pairs={{1,0},{2,1},{3,2},{4,3},{5,4},{6,5},{7,6},{8,7},{9,8},{10,9},{11,1... | collective-permute-start | bytes 245768 | tf_op jit(solution)/shard_map/ppermute | solution.py:439
  105.2 8.3 %copy-start.6 = (f32[20,8,128]{2,1,0:T(8,128)}, f32[20,8,128]{2,1,0:T(8,128)S(1)}, u32[]{:S(2)}) copy-start(f32[20,8,128]{2,1,0:T(8,128)S(1)} %collective-permute-done.4.refs_4_) | copy-start | bytes 245764
  113.4 0.6 copy-start.7

commit v3 on v2

--- a/solution.py
+++ b/solution.py
@@ -14,6 +14,7 @@
 WIDTH = ROWS * 128
 CHUNK = 32
 GROUP = 8
+QUAD = 4
 FIELDS = 8
 PEER_ROWS = FIELDS + 1
 TERMS = 32
@@ -105,7 +106,35 @@
     copy.wait()
 
 
-def unpack_kernel(got_hbm, head, tail, items, starts, count, heads_v, heads_s, store, got, sem):
+def list_kernel(count, fulls, halves, starts):
+    cells = starts.shape[0] - 2
+    for index in range(fulls.shape[0]):
+        fulls[index] = 0
+    for index in range(halves.shape[0]):
+        halves[index] = 0
+
+    def list_cell(cell, carry):
+        full, half = carry
+        fulls[full] = cell
+        halves[half] = cell
+        more = (count[cell] > CHUNK).astype(jnp.int32)
+        starts[cell] = jnp.where(more > 0, 2 * full, -1 - half)
+        return full + more, half + 1 - more
+
+    full, half = lax.fori_loop(0, cells, list_cell, (0, 0), unroll=8)
+    full_turns = (2 * full + GROUP - 1) // GROUP
+    starts[cells] = full_turns
+    starts[cells + 1] = (half + GROUP - 1) // GROUP
+
+    def shift_cell(cell, carry):
+        start = starts[cell]
+        starts[cell] = jnp.where(start < 0, GROUP * full_turns - 1 - start, start)
+        return carry
+
+    lax.fori_loop(0, cells, shift_cell, 0, unroll=8)
+
+
+def unpack_kernel(got_hbm, head, tail, count, heads_v, heads_s, store, got, sem):
     copy = pltpu.make_async_copy(got_hbm, got, sem)
     copy.start()
     copy.wait()
@@ -132,17 +161,6 @@
         return carry
 
     lax.fori_loop(0, peers, take, 0, unroll=8)
-    for index in range(items.shape[0]):
-        items[index] = 0
-
-    def list_items(cell, total):
-        starts[cell] = total
-        items[total] = 2 * cell
-        items[total + 1] = 2 * cell + 1
-        return total + 1 + (count[cell] > CHUNK).astype(jnp.int32)
-
-    total = lax.fori_loop(0, 2 * pairs, list_items, 0, unroll=8)
-    starts[2 * pairs] = (total + GROUP - 1) // GROUP
     head[...] = store[0 : pairs // 2]
     tail[...] = store[pairs // 2 : pairs]
 
@@ -161,13 +179,50 @@
     second[index + 1] = jnp.where(low, zero, tile).astype(first.dtype)
 
 
-def over_items(groups, one_item):
-    def turn(step, carry):
-        for local in range(GROUP):
-            one_item(step, local)
-        return carry
-
-    lax.fori_loop(0, groups, turn, 0)
+def lane_sums(picks, value):
+    total = jnp.zeros((FIELDS, value.shape[0]), F32)
+    for part in split_bf16(value, 2):
+        total = total + lax.dot_general(
+            picks, part.astype(BF16), (((1,), (1,)), ((), ())), preferred_element_type=F32
+        )
+    return total
+
+
+def over_items(lists, cells, one_cell, acc, sums, picks):
+    fulls, halves, starts = lists
+    full_turns = starts[cells]
+    quads = GROUP // QUAD
+
+    def add_up(step):
+        for n in range(quads):
+            sums[step * quads + n] = lane_sums(picks, acc[step * quads + n])
+
+    def turns(chosen, each, skipped):
+        def turn(step, carry):
+            add_up(jnp.maximum(skipped + step - 1, 0))
+            place = (skipped + step) * GROUP
+            values = []
+            for local in range(GROUP // each):
+                cell = chosen[step * (GROUP // each) + local]
+                values += one_cell(cell, place + each * local, local, each)
+            for n, value in enumerate(values):
+                acc[(skipped + step) * quads + n // QUAD, n % QUAD * CHUNK : n % QUAD * CHUNK + CHUNK, :] = value
+            return carry
+
+        return turn
+
+    lax.fori_loop(0, full_turns, turns(fulls, 2, 0), 0)
+    lax.fori_loop(0, starts[cells + 1], turns(halves, 1, full_turns), 0)
+    add_up(full_turns + starts[cells + 1] - 1)
+
+
+def pair_sums(sums, starts, pair, group):
+    total = None
+    for n in range(4):
+        place = starts[2 * pair + n // 2] + n % 2
+        tile = pltpu.roll(sums[place // QUAD], ((n - place) & 3) * CHUNK, 1)
+        total = tile if total is None else jnp.where(group == n, tile, total)
+    return total
 
 
 def entries(adj, cell, dummy):
@@ -175,8 +230,8 @@
 
 
 def density_kernel(
-    items, starts, adj, left, head, tail, right, hi, lo, dens, coef_head, coef_tail,
-    terms_a, terms_b, ext, stage, lhs, own_r, rows_t, rows_f, acc, raw,
+    fulls, halves, starts, adj, left, head, tail, right, h, dens, coef_head, coef_tail,
+    terms_a, terms_b, ext, stage, lhs, own_r, rows_t, rows_f, acc, sums, raw,
 ):
     rim = 2 * head.shape[0]
     quarter = head.shape[0]
@@ -218,58 +273,45 @@
                     stage[at, 24:32, :] = jnp.where(sub8 < 3, extra, tile[7:8])
                     turned = jnp.transpose(stage[at])
                     radius = jnp.broadcast_to(turned[:, 31:32], (128, 128))
-                    lhs[4 * own : 4 * own + 4] = turned.astype(BF16).reshape(4, CHUNK, TERMS)
-                    own_r[4 * own : 4 * own + 4] = radius.reshape(4, CHUNK, 128)
-
-    chunk_lane = lane_iota((CHUNK, 128))
-    chunk_sub = sub_iota((CHUNK, 128))
-
-    def one_item(step, local):
-        place = step * GROUP + local
-        item = items[place]
-        cell = item // 2
-        at = local
+                    lhs[2 * own : 2 * own + 2] = turned.astype(BF16).reshape(2, SLOTS, TERMS)
+                    own_r[2 * own : 2 * own + 2] = radius.reshape(2, SLOTS, 128)
+
+    item_lane = lane_iota((CHUNK, 128))
+    item_sub = sub_iota((CHUNK, 128))
+
+    def one_cell(cell, place, at, each):
         index = entries(adj, cell, dummy)
         for p in range(ROWS):
             i, j = index[2 * p], index[2 * p + 1]
             rows_f[at, p] = jnp.where(low8, ext[i], ext[j])
             rows_t[at, :, p * 128 : p * 128 + 128] = terms_a[i] + terms_b[j]
-        own = lhs[item]
-        ri = own_r[item]
-        first = (item - 2 * cell) * CHUNK
-        total = jnp.zeros((CHUNK, 128), F32)
+        own = lhs[cell, 0 : each * CHUNK]
+        totals = [jnp.zeros((CHUNK, 128), F32) for _ in range(each)]
         for p2 in range(ROWS // 2):
             wide = jnp.dot(
                 own, rows_t[at, :, p2 * 256 : p2 * 256 + 256], preferred_element_type=F32
             )
             for p in (2 * p2, 2 * p2 + 1):
-                q = jnp.maximum(wide[:, (p % 2) * 128 : (p % 2) * 128 + 128], 0.0)
-                q2 = q * q
-                total = total + q2 * (q * rows_f[at, p, 6:7, :])
-                value = q2 * pl.reciprocal(ri + rows_f[at, p, 7:8, :])
-                if p == 0:
-                    value = jnp.where(chunk_lane == chunk_sub + first, 0.0, value)
-                upper = value.astype(BF16)
-                span = slice(p * 128, p * 128 + 128)
-                hi[place, :, span] = upper
-                lo[place, :, span] = (value - upper.astype(F32)).astype(BF16)
-        acc[item] = total
-
-    over_items(starts[4 * quarter], one_item)
+                for part in range(each):
+                    first = part * CHUNK
+                    q = wide[first : first + CHUNK, (p % 2) * 128 : (p % 2) * 128 + 128]
+                    q = jnp.maximum(q, 0.0)
+                    q2 = q * q
+                    totals[part] = totals[part] + q2 * (q * rows_f[at, p, 6:7, :])
+                    ri = own_r[cell, first : first + CHUNK]
+                    value = q2 * pl.reciprocal(ri + rows_f[at, p, 7:8, :])
+                    if p == 0:
+                        value = jnp.where(item_lane == item_sub + first, 0.0, value)
+                    h[place + part, p] = value
+        return totals
+
+    over_items((fulls, halves, starts), 4 * quarter, one_cell, acc, sums, jnp.ones((FIELDS, 128), BF16))
 
     if True:
-        ones = jnp.ones((FIELDS, 128), BF16)
-
-        def reduce_pair(pair, carry):
-            total = jnp.zeros((FIELDS, 128), F32)
-            for part in split_bf16(acc[pl.ds(4 * pair, 4)].reshape(2 * SLOTS, 128), 3):
-                total = total + lax.dot_general(
-                    ones, part.astype(BF16), (((1,), (1,)), ((), ())), preferred_element_type=F32
-                )
-            raw[pl.ds(pair, 1), :] = total[0:1]
-            return carry
-
-        lax.fori_loop(0, 2 * quarter, reduce_pair, 0, unroll=4)
+        group = lane_iota((FIELDS, 128)) // CHUNK
+        for pair in range(2 * quarter):
+            total = pair_sums(sums, starts, pair, group)
+            raw[pair : pair + 1, :] = total[0:1]
         for part, (ref, coef) in enumerate(((head, coef_head), (tail, coef_tail))):
             mass = ref[:, 6, :]
             live = mass > 0.0
@@ -278,67 +320,83 @@
             coef[...] = (2.0 * visc_scale) * mass / jnp.where(live, value, 1.0)
 
 
-def sweep_kernel(is_first, items, starts, adj, hi, lo, *refs):
+def sweep_kernel(is_first, fulls, halves, starts, adj, h, *refs):
     coefs, speeds, refs = refs[:4], refs[4:8], refs[8:]
     if is_first:
-        (head, tail), (out_head, out_tail), refs = speeds[1:3], refs[:2], refs[2:]
+        (head, tail), (out_head, out_tail, below), refs = speeds[1:3], refs[:3], refs[3:]
     else:
-        (head, tail), (out,), refs = refs[:2], refs[2:3], refs[3:]
-    ext_a, ext_b, rows, sums, stage = refs
+        (head, tail, below), (out,), refs = refs[:3], refs[3:4], refs[4:]
+    ext, rows, acc, sums = refs
     quarter = head.shape[0]
     rim = 2 * quarter
     dummy = 4 * rim
-    low = lane_iota((FIELDS, 128)) < SLOTS
-    low16 = lane_iota((2 * FIELDS, 128)) < SLOTS
-    eighth = lane_iota((FIELDS, 128)) // CHUNK
+    lane = lane_iota((FIELDS, 128))
+    low = lane < SLOTS
     sub = sub_iota((FIELDS, 128))
     moving = (sub >= 3) & (sub < 6)
-
-    if True:
-        ext_a[dummy] = jnp.zeros((2 * FIELDS, 128), BF16)
-        ext_b[dummy] = jnp.zeros((2 * FIELDS, 128), BF16)
-        for part in range(4):
-            for pair in range(quarter):
-                tile = jnp.where(sub == 0, 1.0, jnp.where(moving, speeds[part][pair], 0.0))
-                w1, w2 = split_bf16(tile * coefs[part][pair : pair + 1, :], 2)
-                at = pair % 8
-                stage[at, 0:FIELDS, :] = w1
-                stage[at, FIELDS:, :] = w2
-                put_halves(stage[at], low16, ext_a, ext_b, part * rim + 2 * pair)
-
-    def one_item(step, local):
-        place = step * GROUP + local
-        index = entries(adj, items[place] // 2, dummy)
-        at = local
+    ext[dummy] = jnp.zeros((FIELDS, 128), F32)
+    for part in range(4):
+        for pair in range(quarter):
+            tile = jnp.where(sub == 2, 1.0, jnp.where(moving, speeds[part][pair], 0.0))
+            tile = tile * coefs[part][pair : pair + 1, :]
+            turned = pltpu.roll(tile, SLOTS, 1)
+            slot = part * rim + 2 * pair
+            ext[slot] = jnp.where(low, tile, turned)
+            ext[slot + 1] = jnp.where(low, turned, tile)
+    order = (3, 5, 4, 2)
+    item_group = lane_iota((CHUNK, 128)) // CHUNK
+    item_low = item_group < 2
+    item_even = item_group % 2 == 0
+
+    def merge(a, b):
+        if b is None:
+            return a + pltpu.roll(a, 64, 1)
+        return jnp.where(item_low, a, b) + pltpu.roll(jnp.where(item_low, b, a), 64, 1)
+
+    def one_cell(cell, place, at, each):
+        index = entries(adj, cell, dummy)
         for p in range(ROWS):
-            rows[at, :, p * 128 : p * 128 + 128] = ext_a[index[2 * p]] + ext_b[index[2 * p + 1]]
-        total = jnp.zeros((2 * FIELDS, CHUNK), F32)
-        for part in (hi, lo):
-            total = total + lax.dot_general(
-                rows[at], part[place], (((1,), (1,)), ((), ())), preferred_element_type=F32
-            )
-        sums[place, :, 0:CHUNK] = total[0:FIELDS] + total[FIELDS:]
-
-    over_items(starts[2 * rim], one_item)
-
-    if True:
-        for part, ref in enumerate((head, tail)):
-            for pair in range(quarter):
-                slot = part * quarter + pair
-                tile = ref[pair]
-                total = sums[starts[2 * slot]]
-                for n in range(1, 4):
-                    place = starts[2 * slot + n // 2] + n % 2
-                    total = jnp.where(eighth == n, pltpu.roll(sums[place], n * CHUNK, 1), total)
-                live = jnp.broadcast_to(tile[6:7] > 0.0, (FIELDS, 128))
-                rate = mass_rate * tile[6:7]
-                below = jnp.broadcast_to(rate + total[0:1], (FIELDS, 128))
-                value = (rate * tile + total) / jnp.where(live, below, 1.0)
-                value = jnp.where(live & moving, value, 0.0)
-                if is_first:
-                    (out_head, out_tail)[part][pair] = value
-                else:
-                    out[:, slot * 128 : slot * 128 + 128] = value[3:6]
+            rows[at, p] = jnp.where(low, ext[index[2 * p]], ext[index[2 * p + 1]])
+        merged = []
+        for part in range(each):
+            totals = [jnp.zeros((CHUNK, 128), F32) for _ in order]
+            for p in range(ROWS):
+                value = h[place + part, p]
+                for n, f in enumerate(order):
+                    if is_first or f != 2:
+                        totals[n] = totals[n] + value * rows[at, p, f : f + 1, :]
+            even = merge(totals[0], totals[2])
+            odd = merge(totals[1], totals[3] if is_first else None)
+            other = jnp.where(item_even, odd, even)
+            moved = jnp.where(item_even, pltpu.roll(other, 96, 1), pltpu.roll(other, 32, 1))
+            merged.append(jnp.where(item_even, even, odd) + moved)
+        return merged
+
+    group = lane // CHUNK
+    picks = jnp.zeros((FIELDS, 128), jnp.bool_)
+    for n, f in enumerate(order):
+        picks = picks | ((group == n) & (sub == f))
+    picks = picks.astype(F32).astype(BF16)
+    over_items((fulls, halves, starts), 2 * rim, one_cell, acc, sums, picks)
+    for part, ref in enumerate((head, tail)):
+        for pair in range(quarter):
+            slot = part * quarter + pair
+            tile = ref[pair]
+            total = pair_sums(sums, starts, slot, group)
+            if is_first:
+                weight = total[2:3]
+                below[slot : slot + 1, :] = weight
+            else:
+                weight = below[slot : slot + 1, :]
+            live = jnp.broadcast_to(tile[6:7] > 0.0, (FIELDS, 128))
+            rate = mass_rate * tile[6:7]
+            under = jnp.broadcast_to(rate + weight, (FIELDS, 128))
+            value = (rate * tile + total) / jnp.where(live, under, 1.0)
+            value = jnp.where(live & moving, value, 0.0)
+            if is_first:
+                (out_head, out_tail)[part][pair] = value
+            else:
+                out[:, slot * 128 : slot * 128 + 128] = value[3:6]
 
 
 def call(kernel, outs, scratch, in_specs, args, out_specs, grid=(), scalars=0, vmem=40):
@@ -368,7 +426,7 @@
     return pl.BlockSpec(shape, lambda *scalars: (0,) * len(shape))
 
 
-def density(items, starts, adj, left, head, tail, right):
+def density(lists, adj, left, head, tail, right):
     quarter = head.shape[0]
     cells, pairs = 4 * quarter, 2 * quarter
     ext = 2 * cells + 1
@@ -376,52 +434,53 @@
     block = spec(VMEM)
     return call(
         density_kernel,
-        [pltpu.VMEM((2 * cells, CHUNK, WIDTH), BF16)] * 2
+        [pltpu.VMEM((2 * cells + GROUP, ROWS, CHUNK, 128), F32)]
         + [f32(pairs, 128), f32(quarter, 128), f32(quarter, 128)],
         [pltpu.VMEM((ext, TERMS, 128), BF16)] * 2
         + [
             pltpu.VMEM((ext, FIELDS, 128), F32),
             pltpu.VMEM((16, TERMS, 128), F32),
-            pltpu.VMEM((2 * cells, CHUNK, TERMS), BF16),
-            pltpu.VMEM((2 * cells, CHUNK, 128), F32),
+            pltpu.VMEM((cells, SLOTS, TERMS), BF16),
+            pltpu.VMEM((cells, SLOTS, 128), F32),
             pltpu.VMEM((GROUP, TERMS, WIDTH), BF16),
             pltpu.VMEM((GROUP, ROWS, FIELDS, 128), F32),
-            pltpu.VMEM((2 * cells, CHUNK, 128), F32),
+            pltpu.VMEM(((2 * cells + GROUP) // QUAD, 128, 128), F32),
+            pltpu.VMEM(((2 * cells + GROUP) // QUAD + 1, FIELDS, 128), F32),
             pltpu.VMEM((pairs, 128), F32),
         ],
-        [tile] * 4,
-        (items, starts, adj, left, head, tail, right),
-        out_specs=[block] * 2 + [whole(pairs, 128), whole(quarter, 128), whole(quarter, 128)],
+        [spec(VMEM)] * 4,
+        (*lists, adj, left, head, tail, right),
+        out_specs=[block] + [whole(pairs, 128), whole(quarter, 128), whole(quarter, 128)],
         vmem=22,
-        scalars=3,
-    )
-
-
-def sweep(is_first, items, starts, adj, hi, lo, coefs, speeds, head, tail):
-    quarter = head.shape[0]
-    cells = 4 * quarter
+        scalars=4,
+    )
+
+
+def sweep(is_first, lists, adj, h, coefs, speeds, own):
+    quarter = speeds[0].shape[0]
+    cells, pairs = 4 * quarter, 2 * quarter
     ext = 2 * cells + 1
     tile = whole(quarter, FIELDS, 128)
-    block = spec(VMEM)
-    own = () if is_first else (head, tail)
+    own_specs = [tile, tile, whole(pairs, 128)][: len(own)]
     if is_first:
-        outs, out_specs = [f32(quarter, FIELDS, 128)] * 2, [tile] * 2
+        outs = [f32(quarter, FIELDS, 128)] * 2 + [f32(pairs, 128)]
+        out_specs = [tile] * 2 + [whole(pairs, 128)]
     else:
         outs, out_specs = [f32(3, cells * SLOTS)], [whole(3, cells * SLOTS)]
     return call(
         functools.partial(sweep_kernel, is_first),
         outs,
-        [pltpu.VMEM((ext, 2 * FIELDS, 128), BF16)] * 2
-        + [
-            pltpu.VMEM((GROUP, 2 * FIELDS, WIDTH), BF16),
-            pltpu.VMEM((2 * cells + GROUP, FIELDS, 128), F32),
-            pltpu.VMEM((8, 2 * FIELDS, 128), F32),
+        [
+            pltpu.VMEM((ext, FIELDS, 128), F32),
+            pltpu.VMEM((GROUP, ROWS, FIELDS, 128), F32),
+            pltpu.VMEM(((2 * cells + GROUP) // QUAD, 128, 128), F32),
+            pltpu.VMEM(((2 * cells + GROUP) // QUAD + 1, FIELDS, 128), F32),
         ],
-        [block] * 2 + [whole(quarter, 128)] * 4 + [tile] * (4 + len(own)),
-        (items, starts, adj, hi, lo) + tuple(coefs) + tuple(speeds) + own,
+        [spec(VMEM)] * (9 + len(own)),
+        (*lists, adj, h) + tuple(coefs) + tuple(speeds) + own,
         out_specs=out_specs,
         vmem=22,
-        scalars=3,
+        scalars=4,
     )
 
 
@@ -459,12 +518,11 @@
     got = lax.all_to_all(
         sent.reshape(peers, 1, PEER_ROWS * 128), "cells", split_axis=0, concat_axis=0, tiled=True
     )
-    head, tail, items, starts = call(
+    head, tail, count = call(
         unpack_kernel,
         [f32(quarter, FIELDS, 128)] * 2
-        + [jax.ShapeDtypeStruct((n,), jnp.int32) for n in (2 * cells + GROUP, cells + 1)],
+        + [jax.ShapeDtypeStruct((cells + 1,), jnp.int32)],
         [
-            pltpu.SMEM((cells + 1,), jnp.int32),
             pltpu.VMEM((4, 128), jnp.int32),
             pltpu.SMEM((4, 128), jnp.int32),
             pltpu.VMEM((pairs + 1, FIELDS, 128), F32),
@@ -473,21 +531,29 @@
         ],
         [spec(HBM)],
         (got.reshape(peers * PEER_ROWS, 128),),
-        out_specs=[spec(VMEM)] * 2 + [spec(SMEM)] * 2,
+        out_specs=[spec(VMEM)] * 2 + [spec(SMEM)],
     )
     left, right = rims(head, tail)
+    lists = call(
+        list_kernel,
+        [jax.ShapeDtypeStruct((n,), jnp.int32) for n in (cells + GROUP, cells + GROUP, cells + 2)],
+        [],
+        [spec(SMEM)],
+        (count,),
+        out_specs=[spec(SMEM)] * 3,
+    )
     local = adj - (rank * cells - rim).astype(jnp.int32)
     adj = jnp.concatenate([local[13:14], local[:13], local[14:]], axis=0)
-    hi, lo, dens, coef_head, coef_tail = density(items, starts, adj, left, head, tail, right)
-    hi, lo = (pltpu.with_memory_space_constraint(v, VMEM) for v in (hi, lo))
+    h, dens, coef_head, coef_tail = density(lists, adj, left, head, tail, right)
+    h = pltpu.with_memory_space_constraint(h, VMEM)
     coef_left, coef_right = rims(coef_head, coef_tail)
     coefs = (coef_left, coef_head, coef_tail, coef_right)
-    first_head, first_tail = sweep(
-        True, items, starts, adj, hi, lo, coefs, (left, head, tail, right), head, tail
+    first_head, first_tail, below = sweep(
+        True, lists, adj, h, coefs, (left, head, tail, right), ()
     )
     first_left, first_right = rims(first_head, first_tail)
     speeds = (first_left, first_head, first_tail, first_right)
-    (out,) = sweep(False, items, starts, adj, hi, lo, coefs, speeds, head, tail)
+    (out,) = sweep(False, lists, adj, h, coefs, speeds, (head, tail, below))
     return out, dens.reshape(cells * SLOTS)
 
 

time: 129 us -> 123 us (0.953)
  the two profiles are of different devices: /device:TPU:121 before, /device:TPU:6 now
where the time goes in v3:
time: 123 us; the launch traced here: 121 us
  Pallas kernels  58 us (47%)
  starting transfers between devices  42.1 us (34%)
  waiting for transfers between devices  16.4 us (13%)
  local copies, waits for them, and re-layouts  1.87 us (2%)
  other arithmetic  1.33 us (1%)
    pallas_call x6, Pallas kernels, call(): pl.pallas_call(kernel, out_shape=outs, grid_spec=pltpu.PrefetchScalarGrid...  58 us
    ppermute x3, starting transfers between devices, rims(): lax.ppermute(head, 'cells', left_going)  25.9 us
    all_to_all x1, waiting for transfers between devices, body(): lax.all_to_all(sent.reshape(peers, 1, PEER_ROWS * 128), 'cells', split_ax...  12.5 us
    all_to_all x1, starting transfers between devices, body(): lax.all_to_all(sent.reshape(peers, 1, PEER_ROWS * 128), 'cells', split_ax...  10.5 us
    ppermute x3, starting transfers between devices, rims(): lax.ppermute(tail, 'cells', right_going)  5.74 us
    ppermute x3, waiting for transfers between devices, rims(): lax.ppermute(head, 'cells', left_going)  3.53 us
  transfers between devices with their start and end apart: 7, of which 4 were waited for; matrix products, arithmetic and copies ran while one was open for 1% of the time, Pallas kernels for 2%

profile of v3, /device:TPU:6, one launch (start us, length us, event | category | flops | bytes accessed | tf_op | source)
XLA Modules:
  0.0 120.6 jit_solution(1904522595176300682)
XLA Ops:
  0.6 2.7 %shard_map.113 = f32[1152,128]{1,0:T(8,128)} custom-call(s32[80]{0:T(128)} %refs_0_.1, s32[80]{0:T(128)} %refs_1_.1, s32[80]{0:T(128)} %refs_2_.1, f32[3,5120]{1,0:T(4,128)} %refs_3_.1, f32[3,5120]{1,0:T(4,128)} %refs_4_.1, f32[3,5120]{1,0:T(4,128)} %refs_5_.1, f32[40,128]{1,0:T(8,128)} %bitcast.8, f32[40,128]{1,0:T(8,128)} %bitcast.9, f32[40,128]{1,0:T(8,128)} %bitcast.10), custom_call_target="tpu_custom_call" | custom-call | tf_op jit(solution)/shard_map/pallas_call | solution.py:403
  3.4 10.5 %all-to-all-start = ((f32[128,1,1152]{2,1,0:T(1,128)}), f32[128,1,1152]{2,1,0:T(1,128)S(1)}, u32[]{:S(2)}, u32[]{:S(2)}) async-start(f32[128,1,1152]{2,1,0:T(1,128)} %bitcast.7), calls=%async_computation | async-start | bytes 1179648 | tf_op jit(solution)/shard_map/all_to_all | solution.py:518
  13.9 0.7 broadcast_subtract_fusion
  14.6 12.5 %all-to-all-done = f32[128,1,1152]{2,1,0:T(1,128)S(1)} async-done(((f32[128,1,1152]{2,1,0:T(1,128)}), f32[128,1,1152]{2,1,0:T(1,128)S(1)}, u32[]{:S(2)}, u32[]{:S(2)}) %all-to-all-start) | async-done | bytes 589856 | tf_op jit(solution)/shard_map/all_to_all | solution.py:518
  27.1 3.7 %shard_map.114 = (f32[20,8,128]{2,1,0:T(8,128)S(1)}, f32[20,8,128]{2,1,0:T(8,128)S(1)}, s32[81]{0:T(128)S(1)}) custom-call(f32[1152,128]{1,0:T(8,128)S(1)} %bitcast.6), custom_call_target="tpu_custom_call" | custom-call | tf_op jit(solution)/shard_map/pallas_call | solution.py:403
  30.8 0.0 copy-start
  30.8 0.0 copy-start.1
  30.9 1.9 %collective-permute-start = (f32[20,8,128]{2,1,0:T(8,128)S(1)}, f32[20,8,128]{2,1,0:T(8,128)S(1)}, u32[]{:S(2)}, u32[]{:S(2)}) collective-permute-start(f32[20,8,128]{2,1,0:T(8,128)S(1)} %get-tuple-element.19.tail.refs_6_.refs_9_), channel_id=1, source_target_pairs={{0,1},{1,2},{2,3},{3,4},{4,5},{5,6},{6,7},{7,8},{8,9},{9,10},{10,1... | collective-permute-start | bytes 245768 | tf_op jit(solution)/shard_map/ppermute | solution.py:498
  32.8 7.9 %collective-permute-start.1 = (f32[20,8,128]{2,1,0:T(8,128)S(1)}, f32[20,8,128]{2,1,0:T(8,128)S(1)}, u32[]{:S(2)}, u32[]{:S(2)}) collective-permute-start(f32[20,8,128]{2,1,0:T(8,128)S(1)} %get-tuple-element.20.head.refs_5_.refs_8_), channel_id=1, source_target_pairs={{1,0},{2,1},{3,2},{4,3},{5,4},{6,5},{7,6},{8,7},{9,8},{10,9},{11,1... | collective-permute-start | bytes 245768 | tf_op jit(solution)/shard_map/ppermute | solution.py:498
  40.7 0.6 pad_add_fusion.adj
  41.3 2.1 %shard_map.115 = (s32[88]{0:T(128)S(1)}, s32[88]{0:T(128)S(1)}, s32[82]{0:T(128)S(1)}) custom-call(s32[81]{0:T(128)S(1)} %get-tuple-element.15.count), custom_call_target="tpu_custom_call" | custom-call | tf_op jit(solution)/shard_map/pallas_call | solution.py:403
  43.3 0.0 copy-start.2
  43.3 0.0 copy-start.3
  43.3 0.0 copy-start.4
  43.4 0.0 collective-permute-done.left.refs_4_
  43.4 0.0 copy-start.5
  43.4 0.0 collective-permute-done.1.right.refs_7_
  43.4 0.0 copy-start.6
  43.4 0.4 copy-done.2
  43.8 0.0 copy-done.3
  43.8 0.1 copy-done.4
  43.9 0.0 copy-done
  43.9 0.0 copy-done.1
  43.9 0.1 copy-done.5
  44.0 0.0 copy-done.6
  44.0 19.3 %shard_map.116 = (f32[168,14,32,128]{3,2,1,0:T(8,128)S(1)}, f32[40,128]{1,0:T(8,128)}, f32[20,128]{1,0:T(8,128)}, f32[20,128]{1,0:T(8,128)}) custom-call(s32[88]{0:T(128)} %copy-done.2, s32[88]{0:T(128)} %copy-done.3, s32[82]{0:T(128)} %copy-done.4, s32[27,80]{1,0:T(8,128)} %pad_add_fusion.adj, f32[20,8,128]{2,1,0:T(8,128)} %copy-done.5, ...), custom_call_target="tpu_custom_call" | custom-call | tf_op jit(solution)/shard_map/pallas_call | solution.py:403
  63.4 1.9 %collective-permute-start.2 = (f32[20,128]{1,0:T(8,128)}, f32[20,128]{1,0:T(8,128)S(1)}, u32[]{:S(2)}, u32[]{:S(2)}) collective-permute-start(f32[20,128]{1,0:T(8,128)} %get-tuple-element.22.refs_2_), channel_id=1, source_target_pairs={{0,1},{1,2},{2,3},{3,4},{4,5},{5,6},{6,7},{7,8},{8,9},{9,10},{10,1... | collective-permute-start | bytes 30728 | tf_op jit(solution)/shard_map/ppermute | solution.py:498
  65.3 8.8 %collective-permute-start.3 = (f32[20,128]{1,0:T(8,128)}, f32[20,128]{1,0:T(8,128)S(1)}, u32[]{:S(2)}, u32[]{:S(2)}) collective-permute-start(f32[20,128]{1,0:T(8,128)} %get-tuple-element.23.refs_1_), channel_id=1, source_target_pairs={{1,0},{2,1},{3,2},{4,3},{5,4},{6,5},{7,6},{8,7},{9,8},{10,9},{11,1... | collective-permute-start | bytes 30728 | tf_op jit(solution)/shard_map/ppermute | solution.py:498
  74.1 0.0 collective-permute-done.2.refs_0_
  74.1 0.0 copy-start.9
  74.1 1.6 %collective-permute-done.3.refs_3_ = f32[20,128]{1,0:T(8,128)S(1)} collective-permute-done((f32[20,128]{1,0:T(8,128)}, f32[20,128]{1,0:T(8,128)S(1)}, u32[]{:S(2)}, u32[]{:S(2)}) %collective-permute-start.3) | collective-permute-done | bytes 10272 | tf_op jit(solution)/shard_map/ppermute | solution.py:498
  75.7 0.0 copy-start.10
  75.7 0.0 copy-done.9
  75.7 0.6 copy-done.10
  76.3 15.8 %shard_map.117 = (f32[20,8,128]{2,1,0:T(8,128)}, f32[20,8,128]{2,1,0:T(8,128)}, f32[40,128]{1,0:T(8,128)}) custom-call(s32[88]{0:T(128)} %copy-done.2, s32[88]{0:T(128)} %copy-done.3, s32[82]{0:T(128)} %copy-done.4, s32[27,80]{1,0:T(8,128)} %pad_add_fusion.adj, f32[168,14,32,128]{3,2,1,0:T(8,128)S(1)} %get-tuple-element.21.h, f32[20,128]{1,0:T(8,128)} %copy-done.9, ...), custom_call_target="tpu_custom_call" | custom-call | tf_op jit(solution)/shard_map/pallas_call | solution.py:403
  92.1 1.9 %collective-permute-start.4 = (f32[20,8,128]{2,1,0:T(8,128)}, f32[20,8,128]{2,1,0:T(8,128)S(1)}, u32[]{:S(2)}, u32[]{:S(2)}) collective-permute-start(f32[20,8,128]{2,1,0:T(8,128)} %get-tuple-element.24.refs_6_), channel_id=1, source_target_pairs={{0,1},{1,2},{2,3},{3,4},{4,5},{5,6},{6,7},{7,8},{8,9},{9,10},{10,1... | collective-permute-start | bytes 245768 | tf_op jit(solution)/shard_map/ppermute | solution.py:498
  94.0 9.3 %collective-permute-start.5 = (f32[20,8,128]{2,1,0:T(8,128)}, f32[20,8,128]{2,1,0:T(8,128)S(1)}, u32[]{:S(2)}, u32[]{:S(2)}) collective-permute-start(f32[20,8,128]{2,1,0:T(8,128)} %get-tuple-element.25.refs_5_), channel_id=1, source_target_pairs={{1,0},{2,1},{3,2},{4,3},{5,4},{6,5},{7,6},{8,7},{9,8},{10,9},{11,1... | collective-permute-start | bytes 245768 | tf_op jit(solution)/shard_map/ppermute | solution.py:498
  103.3 0.4 collective-permute-done.4.refs_4_
  103.7 0.0 copy-start.7
  103.7 2.0 %collective-permute-done.5.refs_7_ = f32[20,8,128]{2,1,0:T(8,128)S(1)} collective-permute-done((f32[20,8,128]{2,1,0:T(8,128)}, f32[20,8,128]{2,1,0:T(8,128)S(1)}, u32[]{:S(2)}, u32[]{:S(2)}) %collective-permute-start.5) | collective-permute-done | bytes 81952 | tf_op jit(solution)/shard_map/ppermute | solution.py:498
  105.6 0.0 copy-start.8
  105.6 0.0 copy-done.7
  105.6 0.6 copy-done.8
  106.3 14.3 %shard_map.118 = f32[3,5120]{1,0:T(4,128)} custom-call(s32[88]{0:T(128)} %copy-done.2, s32[88]{0:T(128)} %copy-done.3, s32[82]{0:T(128)} %copy-done.4, s32[27,80]{1,0:T(8,128)} %pad_add_fusion.adj, f32[168,14,32,128]{3,2,1,0:T(8,128)S(1)} %get-tuple-element.21.h, f32[20,128]{1,0:T(8,128)} %copy-done.9, f32[20,128]{1,0:T(8,128)} %get-tuple-element.23.refs_1_, ...), custom_call_target="tpu_custom_call" | custom-call | tf_op jit(solution)/shard_map/pallas_call | solution.py:403
  (2 shorter events, 0.0 us)
Async XLA Ops:
  3.4 23.7 %all-to-all-start = ((f32[128,1,1152]{2,1,0:T(1,128)}), f32[128,1,1152]{2,1,0:T(1,128)S(1)}, u32[]{:S(2)}, u32[]{:S(2)}) async-start(f32[128,1,1152]{2,1,0:T(1,128)} %bitcast.7), calls=%async_computation | async-start | bytes 1179648 | tf_op jit(solution)/shard_map/all_to_all | solution.py:518
  30.8 13.1 %copy-start = (f32[20,8,128]{2,1,0:T(8,128)}, f32[20,8,128]{2,1,0:T(8,128)S(1)}, u32[]{:S(2)}) copy-start(f32[20,8,128]{2,1,0:T(8,128)S(1)} %get-tuple-element.20.head.refs_5_.refs_8_) | copy-start | bytes 245764
  30.8 13.1 %copy-start.1 = (f32[20,8,128]{2,1,0:T(8,128)}, f32[20,8,128]{2,1,0:T(8,128)S(1)}, u32[]{:S(2)}) copy-start(f32[20,8,128]{2,1,0:T(8,128)S(1)} %get-tuple-element.19.tail.refs_6_.refs_9_) | copy-start | bytes 245764
  30.9 12.5 %collective-permute-start = (f32[20,8,128]{2,1,0:T(8,128)S(1)}, f32[20,8,128]{2,1,0:T(8,128)S(1)}, u32[]{:S(2)}, u32[]{:S(2)}) collective-permute-start(f32[20,8,128]{2,1,0:T(8,128)S(1)} %get-tuple-element.19.tail.refs_6_.refs_9_), channel_id=1, source_target_pairs={{0,1},{1,2},{2,3},{3,4},{4,5},{5,6},{6,7},{7,8},{8,9},{9,10},{10,1... | collective-permute-start | bytes 245768 | tf_op jit(solution)/shard_map/ppermute | solution.py:498
  32.8 10.6 %collective-permute-start.1 = (f32[20,8,128]{2,1,0:T(8,128)S(1)}, f32[20,8,128]{2,1,0:T(8,128)S(1)}, u32[]{:S(2)}, u32[]{:S(2)}) collective-permute-start(f32[20,8,128]{2,1,0:T(8,128)S(1)} %get-tuple-element.20.head.refs_5_.refs_8_), channel_id=1, source_target_pairs={{1,0},{2,1},{3,2},{4,3},{5,4},{6,5},{7,6},{8,7},{9,8},{10,9},{11,1... | collective-permute-start | bytes 245768 | tf_op jit(solution)/shard_map/ppermute | solution.py:498
  43.3 0.5 copy-start.2
  43.3 0.5 copy-start.3
  43.3 0.6 copy-start.4
  43.4 0.6 copy-start.5
  43.4 0.6 copy-start.6
  63.4 10.7 %collective-permute-start.2 = (f32[20,128]{1,0:T(8,128)}, f32[20,128]{1,0:T(8,128)S(1)}, u32[]{:S(2)}, u32[]{:S(2)}) collective-permute-start(f32[20,128]{1,0:T(8,128)} %get-tuple-element.22.refs_2_), channel_id=1, source_target_pairs={{0,1},{1,2},{2,3},{3,4},{4,5},{5,6},{6,7},{7,8},{8,9},{9,10},{10,1... | collective-permute-start | bytes 30728 | tf_op jit(solution)/shard_map/ppermute | solution.py:498
  65.3 10.4 %collective-permute-start.3 = (f32[20,128]{1,0:T(8,128)}, f32[20,128]{1,0:T(8,128)S(1)}, u32[]{:S(2)}, u32[]{:S(2)}) collective-permute-start(f32[20,128]{1,0:T(8,128)} %get-tuple-element.23.refs_1_), channel_id=1, source_target_pairs={{1,0},{2,1},{3,2},{4,3},{5,4},{6,5},{7,6},{8,7},{9,8},{10,9},{11,1... | collective-permute-start | bytes 30728 | tf_op jit(solution)/shard_map/ppermute | solution.py:498
  74.1 1.6 %copy-start.9 = (f32[20,128]{1,0:T(8,128)}, f32[20,128]{1,0:T(8,128)S(1)}, u32[]{:S(2)}) copy-start(f32[20,128]{1,0:T(8,128)S(1)} %collective-permute-done.2.refs_0_) | copy-start | bytes 30724
  75.7 0.6 copy-start.10
  92.1 11.6 %collective-permute-start.4 = (f32[20,8,128]{2,1,0:T(8,128)}, f32[20,8,128]{2,1,0:T(8,128)S(1)}, u32[]{:S(2)}, u32[]{:S(2)}) collective-permute-start(f32[20,8,128]{2,1,0:T(8,128)} %get-tuple-element.24.refs_6_), channel_id=1, source_target_pairs={{0,1},{1,2},{2,3},{3,4},{4,5},{5,6},{6,7},{7,8},{8,9},{9,10},{10,1... | collective-permute-start | bytes 245768 | tf_op jit(solution)/shard_map/ppermute | solution.py:498
  94.0 11.6 %collective-permute-start.5 = (f32[20,8,128]{2,1,0:T(8,128)}, f32[20,8,128]{2,1,0:T(8,128)S(1)}, u32[]{:S(2)}, u32[]{:S(2)}) collective-permute-start(f32[20,8,128]{2,1,0:T(8,128)} %get-tuple-element.25.refs_5_), channel_id=1, source_target_pairs={{1,0},{2,1},{3,2},{4,3},{5,4},{6,5},{7,6},{8,7},{9,8},{10,9},{11,1... | collective-permute-start | bytes 245768 | tf_op jit(solution)/shard_map/ppermute | solution.py:498
  103.7 2.0 %copy-start.7 = (f32[20,8,128]{2,1,0:T(8,128)}, f32[20,8,128]{2,1,0:T(8,128)S(1)}, u32[]{:S(2)}) copy-start(f32[20,8,128]{2,1,0:T(8,128)S(1)} %collective-permute-done.4.refs_4_) | copy-start | bytes 245764
  105.6 0.6 copy-start.8

commit v4 on v3

--- a/solution.py
+++ b/solution.py
@@ -100,7 +100,7 @@
             )
         return carry
 
-    lax.fori_loop(0, cells // 2, send, 0, unroll=4)
+    lax.fori_loop(0, cells // 2, send, 0, unroll=8)
     copy = pltpu.make_async_copy(out, sent, out_sem)
     copy.start()
     copy.wait()
@@ -160,7 +160,7 @@
             pltpu.store(store.at[slot // 2], value, mask=half_of == side)
         return carry
 
-    lax.fori_loop(0, peers, take, 0, unroll=8)
+    lax.fori_loop(0, peers, take, 0, unroll=32)
     head[...] = store[0 : pairs // 2]
     tail[...] = store[pairs // 2 : pairs]
 
@@ -414,6 +414,10 @@
     )(*args)
 
 
+def on_chip(values):
+    return tuple(pltpu.with_memory_space_constraint(v, VMEM) for v in values)
+
+
 def f32(*shape):
     return jax.ShapeDtypeStruct(shape, F32)
 
@@ -449,7 +453,7 @@
             pltpu.VMEM((pairs, 128), F32),
         ],
         [spec(VMEM)] * 4,
-        (*lists, adj, left, head, tail, right),
+        (*lists, adj, *on_chip((left, head, tail, right))),
         out_specs=[block] + [whole(pairs, 128), whole(quarter, 128), whole(quarter, 128)],
         vmem=22,
         scalars=4,

time: 123 us -> 122 us (level)
  the two profiles are of different devices: /device:TPU:6 before, /device:TPU:121 now
where the time goes in v4:
time: 122 us; the launch traced here: 121 us
  Pallas kernels  58.7 us (48%)
  starting transfers between devices  28.9 us (24%)
  waiting for transfers between devices  28 us (23%)
  local copies, waits for them, and re-layouts  2.8 us (2%)
  other arithmetic  1.33 us (1%)
    pallas_call x6, Pallas kernels, call(): pl.pallas_call(kernel, out_shape=outs, grid_spec=pltpu.PrefetchScalarGrid...  58.7 us
    ppermute x3, waiting for transfers between devices, rims(): lax.ppermute(head, 'cells', left_going)  19.1 us
    ppermute x3, starting transfers between devices, rims(): lax.ppermute(tail, 'cells', right_going)  12.7 us
    all_to_all x1, starting transfers between devices, body(): lax.all_to_all(sent.reshape(peers, 1, PEER_ROWS * 128), 'cells', split_ax...  10 us
    all_to_all x1, waiting for transfers between devices, body(): lax.all_to_all(sent.reshape(peers, 1, PEER_ROWS * 128), 'cells', split_ax...  8.96 us
    ppermute x3, starting transfers between devices, rims(): lax.ppermute(head, 'cells', left_going)  6.23 us
    unnamed x22, local copies, waits for them, and re-layouts  2.79 us
  transfers between devices with their start and end apart: 7, of which 4 were waited for; matrix products, arithmetic and copies ran while one was open for 1% of the time, Pallas kernels for 2%

profile of v4, /device:TPU:121, one launch (start us, length us, event | category | flops | bytes accessed | tf_op | source)
XLA Modules:
  0.0 120.5 jit_solution(1942578912081814204)
XLA Ops:
  0.6 2.6 %shard_map.113 = f32[1152,128]{1,0:T(8,128)} custom-call(s32[80]{0:T(128)} %refs_0_.1, s32[80]{0:T(128)} %refs_1_.1, s32[80]{0:T(128)} %refs_2_.1, f32[3,5120]{1,0:T(4,128)} %refs_3_.1, f32[3,5120]{1,0:T(4,128)} %refs_4_.1, f32[3,5120]{1,0:T(4,128)} %refs_5_.1, f32[40,128]{1,0:T(8,128)} %bitcast.8, f32[40,128]{1,0:T(8,128)} %bitcast.9, f32[40,128]{1,0:T(8,128)} %bitcast.10), custom_call_target="tpu_custom_call" | custom-call | tf_op jit(solution)/shard_map/pallas_call | solution.py:403
  3.2 10.0 %all-to-all-start = ((f32[128,1,1152]{2,1,0:T(1,128)}), f32[128,1,1152]{2,1,0:T(1,128)S(1)}, u32[]{:S(2)}, u32[]{:S(2)}) async-start(f32[128,1,1152]{2,1,0:T(1,128)} %bitcast.7), calls=%async_computation | async-start | bytes 1179648 | tf_op jit(solution)/shard_map/all_to_all | solution.py:522
  13.3 0.7 broadcast_subtract_fusion
  14.0 9.0 %all-to-all-done = f32[128,1,1152]{2,1,0:T(1,128)S(1)} async-done(((f32[128,1,1152]{2,1,0:T(1,128)}), f32[128,1,1152]{2,1,0:T(1,128)S(1)}, u32[]{:S(2)}, u32[]{:S(2)}) %all-to-all-start) | async-done | bytes 589856 | tf_op jit(solution)/shard_map/all_to_all | solution.py:522
  23.0 3.6 %shard_map.114 = (f32[20,8,128]{2,1,0:T(8,128)S(1)}, f32[20,8,128]{2,1,0:T(8,128)S(1)}, s32[81]{0:T(128)S(1)}) custom-call(f32[1152,128]{1,0:T(8,128)S(1)} %bitcast.6), custom_call_target="tpu_custom_call" | custom-call | tf_op jit(solution)/shard_map/pallas_call | solution.py:403
  26.6 0.0 copy-start
  26.6 0.0 copy-start.1
  26.6 6.7 %collective-permute-start = (f32[20,8,128]{2,1,0:T(8,128)S(1)}, f32[20,8,128]{2,1,0:T(8,128)S(1)}, u32[]{:S(2)}, u32[]{:S(2)}) collective-permute-start(f32[20,8,128]{2,1,0:T(8,128)S(1)} %get-tuple-element.19.tail.refs_6_.refs_9_), channel_id=1, source_target_pairs={{0,1},{1,2},{2,3},{3,4},{4,5},{5,6},{6,7},{7,8},{8,9},{9,10},{10,1... | collective-permute-start | bytes 245768 | tf_op jit(solution)/shard_map/ppermute | solution.py:502
  33.2 1.9 %collective-permute-start.1 = (f32[20,8,128]{2,1,0:T(8,128)S(1)}, f32[20,8,128]{2,1,0:T(8,128)S(1)}, u32[]{:S(2)}, u32[]{:S(2)}) collective-permute-start(f32[20,8,128]{2,1,0:T(8,128)S(1)} %get-tuple-element.20.head.refs_5_.refs_8_), channel_id=1, source_target_pairs={{1,0},{2,1},{3,2},{4,3},{5,4},{6,5},{7,6},{8,7},{9,8},{10,9},{11,1... | collective-permute-start | bytes 245768 | tf_op jit(solution)/shard_map/ppermute | solution.py:502
  35.2 0.6 pad_add_fusion.adj
  35.8 2.1 %shard_map.115 = (s32[88]{0:T(128)S(1)}, s32[88]{0:T(128)S(1)}, s32[82]{0:T(128)S(1)}) custom-call(s32[81]{0:T(128)S(1)} %get-tuple-element.15.count), custom_call_target="tpu_custom_call" | custom-call | tf_op jit(solution)/shard_map/pallas_call | solution.py:403
  37.8 0.0 copy-start.4
  37.9 0.5 copy-done.4
  38.3 0.0 copy-start.5
  38.3 0.5 copy-done.5
  38.8 0.0 copy-start.6
  38.8 0.6 copy-done.6
  39.4 0.0 collective-permute-done.left.refs_4_
  39.4 0.0 copy-start.2
  39.4 3.8 %collective-permute-done.1.right.refs_7_ = f32[20,8,128]{2,1,0:T(8,128)S(1)} collective-permute-done((f32[20,8,128]{2,1,0:T(8,128)S(1)}, f32[20,8,128]{2,1,0:T(8,128)S(1)}, u32[]{:S(2)}, u32[]{:S(2)}) %collective-permute-start.1) | collective-permute-done | bytes 81952 | tf_op jit(solution)/shard_map/ppermute | solution.py:502
  43.2 0.0 copy-start.3
  43.2 19.1 %shard_map.116 = (f32[168,14,32,128]{3,2,1,0:T(8,128)S(1)}, f32[40,128]{1,0:T(8,128)}, f32[20,128]{1,0:T(8,128)}, f32[20,128]{1,0:T(8,128)}) custom-call(s32[88]{0:T(128)} %copy-done.4, s32[88]{0:T(128)} %copy-done.5, s32[82]{0:T(128)} %copy-done.6, s32[27,80]{1,0:T(8,128)} %pad_add_fusion.adj, f32[20,8,128]{2,1,0:T(8,128)S(1)} %collective-permute-done.left.refs_4_, ...), custom_call_target="tpu_custom_call" | custom-call | tf_op jit(solution)/shard_map/pallas_call | solution.py:403
  62.3 4.1 %collective-permute-start.2 = (f32[20,128]{1,0:T(8,128)}, f32[20,128]{1,0:T(8,128)S(1)}, u32[]{:S(2)}, u32[]{:S(2)}) collective-permute-start(f32[20,128]{1,0:T(8,128)} %get-tuple-element.22.refs_2_), channel_id=1, source_target_pairs={{0,1},{1,2},{2,3},{3,4},{4,5},{5,6},{6,7},{7,8},{8,9},{9,10},{10,1... | collective-permute-start | bytes 30728 | tf_op jit(solution)/shard_map/ppermute | solution.py:502
  66.4 1.9 %collective-permute-start.3 = (f32[20,128]{1,0:T(8,128)}, f32[20,128]{1,0:T(8,128)S(1)}, u32[]{:S(2)}, u32[]{:S(2)}) collective-permute-start(f32[20,128]{1,0:T(8,128)} %get-tuple-element.23.refs_1_), channel_id=1, source_target_pairs={{1,0},{2,1},{3,2},{4,3},{5,4},{6,5},{7,6},{8,7},{9,8},{10,9},{11,1... | collective-permute-start | bytes 30728 | tf_op jit(solution)/shard_map/ppermute | solution.py:502
  68.3 0.0 collective-permute-done.2.refs_0_
  68.3 0.0 copy-start.9
  68.3 7.5 %collective-permute-done.3.refs_3_ = f32[20,128]{1,0:T(8,128)S(1)} collective-permute-done((f32[20,128]{1,0:T(8,128)}, f32[20,128]{1,0:T(8,128)S(1)}, u32[]{:S(2)}, u32[]{:S(2)}) %collective-permute-start.3) | collective-permute-done | bytes 10272 | tf_op jit(solution)/shard_map/ppermute | solution.py:502
  75.8 0.0 copy-start.10
  75.8 0.0 copy-done
  75.8 0.0 copy-done.1
  75.8 0.0 copy-done.2
  75.8 0.0 copy-done.3
  75.8 0.0 copy-done.9
  75.9 0.6 copy-done.10
  76.4 16.5 %shard_map.117 = (f32[20,8,128]{2,1,0:T(8,128)}, f32[20,8,128]{2,1,0:T(8,128)}, f32[40,128]{1,0:T(8,128)}) custom-call(s32[88]{0:T(128)} %copy-done.4, s32[88]{0:T(128)} %copy-done.5, s32[82]{0:T(128)} %copy-done.6, s32[27,80]{1,0:T(8,128)} %pad_add_fusion.adj, f32[168,14,32,128]{3,2,1,0:T(8,128)S(1)} %get-tuple-element.21.h, f32[20,128]{1,0:T(8,128)} %copy-done.9, ...), custom_call_target="tpu_custom_call" | custom-call | tf_op jit(solution)/shard_map/pallas_call | solution.py:403
  92.9 1.9 %collective-permute-start.4 = (f32[20,8,128]{2,1,0:T(8,128)}, f32[20,8,128]{2,1,0:T(8,128)S(1)}, u32[]{:S(2)}, u32[]{:S(2)}) collective-permute-start(f32[20,8,128]{2,1,0:T(8,128)} %get-tuple-element.24.refs_6_), channel_id=1, source_target_pairs={{0,1},{1,2},{2,3},{3,4},{4,5},{5,6},{6,7},{7,8},{8,9},{9,10},{10,1... | collective-permute-start | bytes 245768 | tf_op jit(solution)/shard_map/ppermute | solution.py:502
  94.9 2.4 %collective-permute-start.5 = (f32[20,8,128]{2,1,0:T(8,128)}, f32[20,8,128]{2,1,0:T(8,128)S(1)}, u32[]{:S(2)}, u32[]{:S(2)}) collective-permute-start(f32[20,8,128]{2,1,0:T(8,128)} %get-tuple-element.25.refs_5_), channel_id=1, source_target_pairs={{1,0},{2,1},{3,2},{4,3},{5,4},{6,5},{7,6},{8,7},{9,8},{10,9},{11,1... | collective-permute-start | bytes 245768 | tf_op jit(solution)/shard_map/ppermute | solution.py:502
  97.3 0.0 collective-permute-done.4.refs_4_
  97.3 0.0 copy-start.7
  97.3 7.8 %collective-permute-done.5.refs_7_ = f32[20,8,128]{2,1,0:T(8,128)S(1)} collective-permute-done((f32[20,8,128]{2,1,0:T(8,128)}, f32[20,8,128]{2,1,0:T(8,128)S(1)}, u32[]{:S(2)}, u32[]{:S(2)}) %collective-permute-start.5) | collective-permute-done | bytes 81952 | tf_op jit(solution)/shard_map/ppermute | solution.py:502
  105.1 0.0 copy-start.8
  105.1 0.0 copy-done.7
  105.1 0.6 copy-done.8
  105.7 14.8 %shard_map.118 = f32[3,5120]{1,0:T(4,128)} custom-call(s32[88]{0:T(128)} %copy-done.4, s32[88]{0:T(128)} %copy-done.5, s32[82]{0:T(128)} %copy-done.6, s32[27,80]{1,0:T(8,128)} %pad_add_fusion.adj, f32[168,14,32,128]{3,2,1,0:T(8,128)S(1)} %get-tuple-element.21.h, f32[20,128]{1,0:T(8,128)} %copy-done.9, f32[20,128]{1,0:T(8,128)} %get-tuple-element.23.refs_1_, ...), custom_call_target="tpu_custom_call" | custom-call | tf_op jit(solution)/shard_map/pallas_call | solution.py:403
  (2 shorter events, 0.0 us)
Async XLA Ops:
  3.2 19.7 %all-to-all-start = ((f32[128,1,1152]{2,1,0:T(1,128)}), f32[128,1,1152]{2,1,0:T(1,128)S(1)}, u32[]{:S(2)}, u32[]{:S(2)}) async-start(f32[128,1,1152]{2,1,0:T(1,128)} %bitcast.7), calls=%async_computation | async-start | bytes 1179648 | tf_op jit(solution)/shard_map/all_to_all | solution.py:522
  26.6 49.3 %copy-start = (f32[20,8,128]{2,1,0:T(8,128)}, f32[20,8,128]{2,1,0:T(8,128)S(1)}, u32[]{:S(2)}) copy-start(f32[20,8,128]{2,1,0:T(8,128)S(1)} %get-tuple-element.20.head.refs_5_.refs_8_) | copy-start | bytes 245764
  26.6 49.3 %copy-start.1 = (f32[20,8,128]{2,1,0:T(8,128)}, f32[20,8,128]{2,1,0:T(8,128)S(1)}, u32[]{:S(2)}) copy-start(f32[20,8,128]{2,1,0:T(8,128)S(1)} %get-tuple-element.19.tail.refs_6_.refs_9_) | copy-start | bytes 245764
  26.6 12.8 %collective-permute-start = (f32[20,8,128]{2,1,0:T(8,128)S(1)}, f32[20,8,128]{2,1,0:T(8,128)S(1)}, u32[]{:S(2)}, u32[]{:S(2)}) collective-permute-start(f32[20,8,128]{2,1,0:T(8,128)S(1)} %get-tuple-element.19.tail.refs_6_.refs_9_), channel_id=1, source_target_pairs={{0,1},{1,2},{2,3},{3,4},{4,5},{5,6},{6,7},{7,8},{8,9},{9,10},{10,1... | collective-permute-start | bytes 245768 | tf_op jit(solution)/shard_map/ppermute | solution.py:502
  33.2 10.0 %collective-permute-start.1 = (f32[20,8,128]{2,1,0:T(8,128)S(1)}, f32[20,8,128]{2,1,0:T(8,128)S(1)}, u32[]{:S(2)}, u32[]{:S(2)}) collective-permute-start(f32[20,8,128]{2,1,0:T(8,128)S(1)} %get-tuple-element.20.head.refs_5_.refs_8_), channel_id=1, source_target_pairs={{1,0},{2,1},{3,2},{4,3},{5,4},{6,5},{7,6},{8,7},{9,8},{10,9},{11,1... | collective-permute-start | bytes 245768 | tf_op jit(solution)/shard_map/ppermute | solution.py:502
  37.8 0.5 copy-start.4
  38.3 0.5 copy-start.5
  38.8 0.6 copy-start.6
  39.4 36.4 %copy-start.2 = (f32[20,8,128]{2,1,0:T(8,128)}, f32[20,8,128]{2,1,0:T(8,128)S(1)}, u32[]{:S(2)}) copy-start(f32[20,8,128]{2,1,0:T(8,128)S(1)} %collective-permute-done.left.refs_4_) | copy-start | bytes 245764
  43.2 32.6 %copy-start.3 = (f32[20,8,128]{2,1,0:T(8,128)}, f32[20,8,128]{2,1,0:T(8,128)S(1)}, u32[]{:S(2)}) copy-start(f32[20,8,128]{2,1,0:T(8,128)S(1)} %collective-permute-done.1.right.refs_7_) | copy-start | bytes 245764
  62.3 6.0 %collective-permute-start.2 = (f32[20,128]{1,0:T(8,128)}, f32[20,128]{1,0:T(8,128)S(1)}, u32[]{:S(2)}, u32[]{:S(2)}) collective-permute-start(f32[20,128]{1,0:T(8,128)} %get-tuple-element.22.refs_2_), channel_id=1, source_target_pairs={{0,1},{1,2},{2,3},{3,4},{4,5},{5,6},{6,7},{7,8},{8,9},{9,10},{10,1... | collective-permute-start | bytes 30728 | tf_op jit(solution)/shard_map/ppermute | solution.py:502
  66.4 9.4 %collective-permute-start.3 = (f32[20,128]{1,0:T(8,128)}, f32[20,128]{1,0:T(8,128)S(1)}, u32[]{:S(2)}, u32[]{:S(2)}) collective-permute-start(f32[20,128]{1,0:T(8,128)} %get-tuple-element.23.refs_1_), channel_id=1, source_target_pairs={{1,0},{2,1},{3,2},{4,3},{5,4},{6,5},{7,6},{8,7},{9,8},{10,9},{11,1... | collective-permute-start | bytes 30728 | tf_op jit(solution)/shard_map/ppermute | solution.py:502
  68.3 7.5 %copy-start.9 = (f32[20,128]{1,0:T(8,128)}, f32[20,128]{1,0:T(8,128)S(1)}, u32[]{:S(2)}) copy-start(f32[20,128]{1,0:T(8,128)S(1)} %collective-permute-done.2.refs_0_) | copy-start | bytes 30724
  75.8 0.6 copy-start.10
  92.9 4.3 %collective-permute-start.4 = (f32[20,8,128]{2,1,0:T(8,128)}, f32[20,8,128]{2,1,0:T(8,128)S(1)}, u32[]{:S(2)}, u32[]{:S(2)}) collective-permute-start(f32[20,8,128]{2,1,0:T(8,128)} %get-tuple-element.24.refs_6_), channel_id=1, source_target_pairs={{0,1},{1,2},{2,3},{3,4},{4,5},{5,6},{6,7},{7,8},{8,9},{9,10},{10,1... | collective-permute-start | bytes 245768 | tf_op jit(solution)/shard_map/ppermute | solution.py:502
  94.9 10.2 %collective-permute-start.5 = (f32[20,8,128]{2,1,0:T(8,128)}, f32[20,8,128]{2,1,0:T(8,128)S(1)}, u32[]{:S(2)}, u32[]{:S(2)}) collective-permute-start(f32[20,8,128]{2,1,0:T(8,128)} %get-tuple-element.25.refs_5_), channel_id=1, source_target_pairs={{1,0},{2,1},{3,2},{4,3},{5,4},{6,5},{7,6},{8,7},{9,8},{10,9},{11,1... | collective-permute-start | bytes 245768 | tf_op jit(solution)/shard_map/ppermute | solution.py:502
  97.3 7.8 %copy-start.7 = (f32[20,8,128]{2,1,0:T(8,128)}, f32[20,8,128]{2,1,0:T(8,128)S(1)}, u32[]{:S(2)}) copy-start(f32[20,8,128]{2,1,0:T(8,128)S(1)} %collective-permute-done.4.refs_4_) | copy-start | bytes 245764
  105.1 0.6 copy-start.8

commit v5 on v4

--- a/solution.py
+++ b/solution.py
@@ -67,7 +67,7 @@
         out[pl.ds(index * PEER_ROWS + FIELDS, 1), :] = jnp.full((1, 128), -1.0, F32)
         return carry
 
-    lax.fori_loop(0, peers, clear, 0, unroll=8)
+    lax.fori_loop(0, peers, clear, 0, unroll=32)
     for copy in copies:
         copy.wait()
     open_bound = 1.0 - share[...] / jamming_bound
@@ -100,7 +100,7 @@
             )
         return carry
 
-    lax.fori_loop(0, cells // 2, send, 0, unroll=8)
+    lax.fori_loop(0, cells // 2, send, 0, unroll=20)
     copy = pltpu.make_async_copy(out, sent, out_sem)
     copy.start()
     copy.wait()
@@ -160,7 +160,7 @@
             pltpu.store(store.at[slot // 2], value, mask=half_of == side)
         return carry
 
-    lax.fori_loop(0, peers, take, 0, unroll=32)
+    lax.fori_loop(0, peers, take, 0, unroll=64)
     head[...] = store[0 : pairs // 2]
     tail[...] = store[pairs // 2 : pairs]
 

time: 122 us -> 122 us (level); the launches traced: 121 us -> 122 us
  starting transfers between devices: 28.9 us -> 30.2 us
    ppermute x3, starting transfers between devices: 12.7 us -> 14.4 us  [rims(): lax.ppermute(tail, 'cells', right_going)]
where the time goes in v5:
time: 122 us
  Pallas kernels  58.2 us (48%)
  starting transfers between devices  30.2 us (25%)
  waiting for transfers between devices  28.5 us (23%)
  local copies, waits for them, and re-layouts  2.8 us (2%)
  other arithmetic  1.33 us (1%)
    pallas_call x6, Pallas kernels, call(): pl.pallas_call(kernel, out_shape=outs, grid_spec=pltpu.PrefetchScalarGrid...  58.2 us
    ppermute x3, waiting for transfers between devices, rims(): lax.ppermute(head, 'cells', left_going)  19.5 us
    ppermute x3, starting transfers between devices, rims(): lax.ppermute(tail, 'cells', right_going)  14.4 us
    all_to_all x1, starting transfers between devices, body(): lax.all_to_all(sent.reshape(peers, 1, PEER_ROWS * 128), 'cells', split_ax...  10 us
    all_to_all x1, waiting for transfers between devices, body(): lax.all_to_all(sent.reshape(peers, 1, PEER_ROWS * 128), 'cells', split_ax...  8.96 us
    ppermute x3, starting transfers between devices, rims(): lax.ppermute(head, 'cells', left_going)  5.76 us
    unnamed x22, local copies, waits for them, and re-layouts  2.79 us
  transfers between devices with their start and end apart: 7, of which 4 were waited for; matrix products, arithmetic and copies ran while one was open for 1% of the time, Pallas kernels for 2%

profile of v5, /device:TPU:121, one launch (start us, length us, event | category | flops | bytes accessed | tf_op | source)
XLA Modules:
  0.0 121.8 jit_solution(12529014291090746107)
XLA Ops:
  0.6 2.4 %shard_map.113 = f32[1152,128]{1,0:T(8,128)} custom-call(s32[80]{0:T(128)} %refs_0_.1, s32[80]{0:T(128)} %refs_1_.1, s32[80]{0:T(128)} %refs_2_.1, f32[3,5120]{1,0:T(4,128)} %refs_3_.1, f32[3,5120]{1,0:T(4,128)} %refs_4_.1, f32[3,5120]{1,0:T(4,128)} %refs_5_.1, f32[40,128]{1,0:T(8,128)} %bitcast.8, f32[40,128]{1,0:T(8,128)} %bitcast.9, f32[40,128]{1,0:T(8,128)} %bitcast.10), custom_call_target="tpu_custom_call" | custom-call | tf_op jit(solution)/shard_map/pallas_call | solution.py:403
  3.1 10.0 %all-to-all-start = ((f32[128,1,1152]{2,1,0:T(1,128)}), f32[128,1,1152]{2,1,0:T(1,128)S(1)}, u32[]{:S(2)}, u32[]{:S(2)}) async-start(f32[128,1,1152]{2,1,0:T(1,128)} %bitcast.7), calls=%async_computation | async-start | bytes 1179648 | tf_op jit(solution)/shard_map/all_to_all | solution.py:522
  13.1 0.7 broadcast_subtract_fusion
  13.8 9.0 %all-to-all-done = f32[128,1,1152]{2,1,0:T(1,128)S(1)} async-done(((f32[128,1,1152]{2,1,0:T(1,128)}), f32[128,1,1152]{2,1,0:T(1,128)S(1)}, u32[]{:S(2)}, u32[]{:S(2)}) %all-to-all-start) | async-done | bytes 589856 | tf_op jit(solution)/shard_map/all_to_all | solution.py:522
  22.8 3.6 %shard_map.114 = (f32[20,8,128]{2,1,0:T(8,128)S(1)}, f32[20,8,128]{2,1,0:T(8,128)S(1)}, s32[81]{0:T(128)S(1)}) custom-call(f32[1152,128]{1,0:T(8,128)S(1)} %bitcast.6), custom_call_target="tpu_custom_call" | custom-call | tf_op jit(solution)/shard_map/pallas_call | solution.py:403
  26.4 0.0 copy-start
  26.4 0.0 copy-start.1
  26.4 6.7 %collective-permute-start = (f32[20,8,128]{2,1,0:T(8,128)S(1)}, f32[20,8,128]{2,1,0:T(8,128)S(1)}, u32[]{:S(2)}, u32[]{:S(2)}) collective-permute-start(f32[20,8,128]{2,1,0:T(8,128)S(1)} %get-tuple-element.19.tail.refs_6_.refs_9_), channel_id=1, source_target_pairs={{0,1},{1,2},{2,3},{3,4},{4,5},{5,6},{6,7},{7,8},{8,9},{9,10},{10,1... | collective-permute-start | bytes 245768 | tf_op jit(solution)/shard_map/ppermute | solution.py:502
  33.0 1.9 %collective-permute-start.1 = (f32[20,8,128]{2,1,0:T(8,128)S(1)}, f32[20,8,128]{2,1,0:T(8,128)S(1)}, u32[]{:S(2)}, u32[]{:S(2)}) collective-permute-start(f32[20,8,128]{2,1,0:T(8,128)S(1)} %get-tuple-element.20.head.refs_5_.refs_8_), channel_id=1, source_target_pairs={{1,0},{2,1},{3,2},{4,3},{5,4},{6,5},{7,6},{8,7},{9,8},{10,9},{11,1... | collective-permute-start | bytes 245768 | tf_op jit(solution)/shard_map/ppermute | solution.py:502
  35.0 0.6 pad_add_fusion.adj
  35.6 2.1 %shard_map.115 = (s32[88]{0:T(128)S(1)}, s32[88]{0:T(128)S(1)}, s32[82]{0:T(128)S(1)}) custom-call(s32[81]{0:T(128)S(1)} %get-tuple-element.15.count), custom_call_target="tpu_custom_call" | custom-call | tf_op jit(solution)/shard_map/pallas_call | solution.py:403
  37.6 0.0 copy-start.4
  37.7 0.5 copy-done.4
  38.1 0.0 copy-start.5
  38.1 0.5 copy-done.5
  38.6 0.0 copy-start.6
  38.6 0.6 copy-done.6
  39.2 0.0 collective-permute-done.left.refs_4_
  39.2 0.0 copy-start.2
  39.2 3.8 %collective-permute-done.1.right.refs_7_ = f32[20,8,128]{2,1,0:T(8,128)S(1)} collective-permute-done((f32[20,8,128]{2,1,0:T(8,128)S(1)}, f32[20,8,128]{2,1,0:T(8,128)S(1)}, u32[]{:S(2)}, u32[]{:S(2)}) %collective-permute-start.1) | collective-permute-done | bytes 81952 | tf_op jit(solution)/shard_map/ppermute | solution.py:502
  43.0 0.0 copy-start.3
  43.0 18.9 %shard_map.116 = (f32[168,14,32,128]{3,2,1,0:T(8,128)S(1)}, f32[40,128]{1,0:T(8,128)}, f32[20,128]{1,0:T(8,128)}, f32[20,128]{1,0:T(8,128)}) custom-call(s32[88]{0:T(128)} %copy-done.4, s32[88]{0:T(128)} %copy-done.5, s32[82]{0:T(128)} %copy-done.6, s32[27,80]{1,0:T(8,128)} %pad_add_fusion.adj, f32[20,8,128]{2,1,0:T(8,128)S(1)} %collective-permute-done.left.refs_4_, ...), custom_call_target="tpu_custom_call" | custom-call | tf_op jit(solution)/shard_map/pallas_call | solution.py:403
  61.9 5.1 %collective-permute-start.2 = (f32[20,128]{1,0:T(8,128)}, f32[20,128]{1,0:T(8,128)S(1)}, u32[]{:S(2)}, u32[]{:S(2)}) collective-permute-start(f32[20,128]{1,0:T(8,128)} %get-tuple-element.22.refs_2_), channel_id=1, source_target_pairs={{0,1},{1,2},{2,3},{3,4},{4,5},{5,6},{6,7},{7,8},{8,9},{9,10},{10,1... | collective-permute-start | bytes 30728 | tf_op jit(solution)/shard_map/ppermute | solution.py:502
  67.0 1.9 %collective-permute-start.3 = (f32[20,128]{1,0:T(8,128)}, f32[20,128]{1,0:T(8,128)S(1)}, u32[]{:S(2)}, u32[]{:S(2)}) collective-permute-start(f32[20,128]{1,0:T(8,128)} %get-tuple-element.23.refs_1_), channel_id=1, source_target_pairs={{1,0},{2,1},{3,2},{4,3},{5,4},{6,5},{7,6},{8,7},{9,8},{10,9},{11,1... | collective-permute-start | bytes 30728 | tf_op jit(solution)/shard_map/ppermute | solution.py:502
  68.9 0.0 collective-permute-done.2.refs_0_
  68.9 0.0 copy-start.9
  69.0 7.5 %collective-permute-done.3.refs_3_ = f32[20,128]{1,0:T(8,128)S(1)} collective-permute-done((f32[20,128]{1,0:T(8,128)}, f32[20,128]{1,0:T(8,128)S(1)}, u32[]{:S(2)}, u32[]{:S(2)}) %collective-permute-start.3) | collective-permute-done | bytes 10272 | tf_op jit(solution)/shard_map/ppermute | solution.py:502
  76.4 0.0 copy-start.10
  76.4 0.0 copy-done
  76.5 0.0 copy-done.1
  76.5 0.0 copy-done.2
  76.5 0.0 copy-done.3
  76.5 0.0 copy-done.9
  76.5 0.6 copy-done.10
  77.0 16.5 %shard_map.117 = (f32[20,8,128]{2,1,0:T(8,128)}, f32[20,8,128]{2,1,0:T(8,128)}, f32[40,128]{1,0:T(8,128)}) custom-call(s32[88]{0:T(128)} %copy-done.4, s32[88]{0:T(128)} %copy-done.5, s32[82]{0:T(128)} %copy-done.6, s32[27,80]{1,0:T(8,128)} %pad_add_fusion.adj, f32[168,14,32,128]{3,2,1,0:T(8,128)S(1)} %get-tuple-element.21.h, f32[20,128]{1,0:T(8,128)} %copy-done.9, ...), custom_call_target="tpu_custom_call" | custom-call | tf_op jit(solution)/shard_map/pallas_call | solution.py:403
  93.5 2.7 %collective-permute-start.4 = (f32[20,8,128]{2,1,0:T(8,128)}, f32[20,8,128]{2,1,0:T(8,128)S(1)}, u32[]{:S(2)}, u32[]{:S(2)}) collective-permute-start(f32[20,8,128]{2,1,0:T(8,128)} %get-tuple-element.24.refs_6_), channel_id=1, source_target_pairs={{0,1},{1,2},{2,3},{3,4},{4,5},{5,6},{6,7},{7,8},{8,9},{9,10},{10,1... | collective-permute-start | bytes 245768 | tf_op jit(solution)/shard_map/ppermute | solution.py:502
  96.2 1.9 %collective-permute-start.5 = (f32[20,8,128]{2,1,0:T(8,128)}, f32[20,8,128]{2,1,0:T(8,128)S(1)}, u32[]{:S(2)}, u32[]{:S(2)}) collective-permute-start(f32[20,8,128]{2,1,0:T(8,128)} %get-tuple-element.25.refs_5_), channel_id=1, source_target_pairs={{1,0},{2,1},{3,2},{4,3},{5,4},{6,5},{7,6},{8,7},{9,8},{10,9},{11,1... | collective-permute-start | bytes 245768 | tf_op jit(solution)/shard_map/ppermute | solution.py:502
  98.2 0.0 collective-permute-done.4.refs_4_
  98.2 0.0 copy-start.7
  98.2 8.2 %collective-permute-done.5.refs_7_ = f32[20,8,128]{2,1,0:T(8,128)S(1)} collective-permute-done((f32[20,8,128]{2,1,0:T(8,128)}, f32[20,8,128]{2,1,0:T(8,128)S(1)}, u32[]{:S(2)}, u32[]{:S(2)}) %collective-permute-start.5) | collective-permute-done | bytes 81952 | tf_op jit(solution)/shard_map/ppermute | solution.py:502
  106.4 0.0 copy-start.8
  106.4 0.0 copy-done.7
  106.4 0.6 copy-done.8
  107.1 14.8 %shard_map.118 = f32[3,5120]{1,0:T(4,128)} custom-call(s32[88]{0:T(128)} %copy-done.4, s32[88]{0:T(128)} %copy-done.5, s32[82]{0:T(128)} %copy-done.6, s32[27,80]{1,0:T(8,128)} %pad_add_fusion.adj, f32[168,14,32,128]{3,2,1,0:T(8,128)S(1)} %get-tuple-element.21.h, f32[20,128]{1,0:T(8,128)} %copy-done.9, f32[20,128]{1,0:T(8,128)} %get-tuple-element.23.refs_1_, ...), custom_call_target="tpu_custom_call" | custom-call | tf_op jit(solution)/shard_map/pallas_call | solution.py:403
  (2 shorter events, 0.0 us)
Async XLA Ops:
  3.1 19.7 %all-to-all-start = ((f32[128,1,1152]{2,1,0:T(1,128)}), f32[128,1,1152]{2,1,0:T(1,128)S(1)}, u32[]{:S(2)}, u32[]{:S(2)}) async-start(f32[128,1,1152]{2,1,0:T(1,128)} %bitcast.7), calls=%async_computation | async-start | bytes 1179648 | tf_op jit(solution)/shard_map/all_to_all | solution.py:522
  26.4 50.1 %copy-start = (f32[20,8,128]{2,1,0:T(8,128)}, f32[20,8,128]{2,1,0:T(8,128)S(1)}, u32[]{:S(2)}) copy-start(f32[20,8,128]{2,1,0:T(8,128)S(1)} %get-tuple-element.20.head.refs_5_.refs_8_) | copy-start | bytes 245764
  26.4 50.1 %copy-start.1 = (f32[20,8,128]{2,1,0:T(8,128)}, f32[20,8,128]{2,1,0:T(8,128)S(1)}, u32[]{:S(2)}) copy-start(f32[20,8,128]{2,1,0:T(8,128)S(1)} %get-tuple-element.19.tail.refs_6_.refs_9_) | copy-start | bytes 245764
  26.4 12.8 %collective-permute-start = (f32[20,8,128]{2,1,0:T(8,128)S(1)}, f32[20,8,128]{2,1,0:T(8,128)S(1)}, u32[]{:S(2)}, u32[]{:S(2)}) collective-permute-start(f32[20,8,128]{2,1,0:T(8,128)S(1)} %get-tuple-element.19.tail.refs_6_.refs_9_), channel_id=1, source_target_pairs={{0,1},{1,2},{2,3},{3,4},{4,5},{5,6},{6,7},{7,8},{8,9},{9,10},{10,1... | collective-permute-start | bytes 245768 | tf_op jit(solution)/shard_map/ppermute | solution.py:502
  33.0 10.0 %collective-permute-start.1 = (f32[20,8,128]{2,1,0:T(8,128)S(1)}, f32[20,8,128]{2,1,0:T(8,128)S(1)}, u32[]{:S(2)}, u32[]{:S(2)}) collective-permute-start(f32[20,8,128]{2,1,0:T(8,128)S(1)} %get-tuple-element.20.head.refs_5_.refs_8_), channel_id=1, source_target_pairs={{1,0},{2,1},{3,2},{4,3},{5,4},{6,5},{7,6},{8,7},{9,8},{10,9},{11,1... | collective-permute-start | bytes 245768 | tf_op jit(solution)/shard_map/ppermute | solution.py:502
  37.6 0.5 copy-start.4
  38.1 0.5 copy-start.5
  38.6 0.6 copy-start.6
  39.2 37.2 %copy-start.2 = (f32[20,8,128]{2,1,0:T(8,128)}, f32[20,8,128]{2,1,0:T(8,128)S(1)}, u32[]{:S(2)}) copy-start(f32[20,8,128]{2,1,0:T(8,128)S(1)} %collective-permute-done.left.refs_4_) | copy-start | bytes 245764
  43.0 33.4 %copy-start.3 = (f32[20,8,128]{2,1,0:T(8,128)}, f32[20,8,128]{2,1,0:T(8,128)S(1)}, u32[]{:S(2)}) copy-start(f32[20,8,128]{2,1,0:T(8,128)S(1)} %collective-permute-done.1.right.refs_7_) | copy-start | bytes 245764
  61.9 7.0 %collective-permute-start.2 = (f32[20,128]{1,0:T(8,128)}, f32[20,128]{1,0:T(8,128)S(1)}, u32[]{:S(2)}, u32[]{:S(2)}) collective-permute-start(f32[20,128]{1,0:T(8,128)} %get-tuple-element.22.refs_2_), channel_id=1, source_target_pairs={{0,1},{1,2},{2,3},{3,4},{4,5},{5,6},{6,7},{7,8},{8,9},{9,10},{10,1... | collective-permute-start | bytes 30728 | tf_op jit(solution)/shard_map/ppermute | solution.py:502
  67.0 9.4 %collective-permute-start.3 = (f32[20,128]{1,0:T(8,128)}, f32[20,128]{1,0:T(8,128)S(1)}, u32[]{:S(2)}, u32[]{:S(2)}) collective-permute-start(f32[20,128]{1,0:T(8,128)} %get-tuple-element.23.refs_1_), channel_id=1, source_target_pairs={{1,0},{2,1},{3,2},{4,3},{5,4},{6,5},{7,6},{8,7},{9,8},{10,9},{11,1... | collective-permute-start | bytes 30728 | tf_op jit(solution)/shard_map/ppermute | solution.py:502
  68.9 7.5 %copy-start.9 = (f32[20,128]{1,0:T(8,128)}, f32[20,128]{1,0:T(8,128)S(1)}, u32[]{:S(2)}) copy-start(f32[20,128]{1,0:T(8,128)S(1)} %collective-permute-done.2.refs_0_) | copy-start | bytes 30724
  76.4 0.6 copy-start.10
  93.5 4.6 %collective-permute-start.4 = (f32[20,8,128]{2,1,0:T(8,128)}, f32[20,8,128]{2,1,0:T(8,128)S(1)}, u32[]{:S(2)}, u32[]{:S(2)}) collective-permute-start(f32[20,8,128]{2,1,0:T(8,128)} %get-tuple-element.24.refs_6_), channel_id=1, source_target_pairs={{0,1},{1,2},{2,3},{3,4},{4,5},{5,6},{6,7},{7,8},{8,9},{9,10},{10,1... | collective-permute-start | bytes 245768 | tf_op jit(solution)/shard_map/ppermute | solution.py:502
  96.2 10.2 %collective-permute-start.5 = (f32[20,8,128]{2,1,0:T(8,128)}, f32[20,8,128]{2,1,0:T(8,128)S(1)}, u32[]{:S(2)}, u32[]{:S(2)}) collective-permute-start(f32[20,8,128]{2,1,0:T(8,128)} %get-tuple-element.25.refs_5_), channel_id=1, source_target_pairs={{1,0},{2,1},{3,2},{4,3},{5,4},{6,5},{7,6},{8,7},{9,8},{10,9},{11,1... | collective-permute-start | bytes 245768 | tf_op jit(solution)/shard_map/ppermute | solution.py:502
  98.2 8.3 %copy-start.7 = (f32[20,8,128]{2,1,0:T(8,128)}, f32[20,8,128]{2,1,0:T(8,128)S(1)}, u32[]{:S(2)}) copy-start(f32[20,8,128]{2,1,0:T(8,128)S(1)} %collective-permute-done.4.refs_4_) | copy-start | bytes 245764
  106.4 0.6 copy-start.8
